TPU v7x, 512 devices: a whole 4x4x16 slice. The times are simulated.
512 devices in a mesh: dp: 16 (over y, x), expert: 32 (over z, core).
Axes of the slice: x: 4, y: 4, z: 16, core: 2. Of those that a mesh axis runs over, the one named last changes fastest.
Arguments:
- tokens: bfloat16 [2048, 5120], P(('dp', 'expert')), may hold values from -6 to 6
- chosen_expert_index: int32 [2048, 6], P(('dp', 'expert')), may hold values from 0 to 31, all different within a row; in each aligned block of 4 rows (0 to 3, 4 to 7, ...) at most 2 rows name the same one
- router_gate_weight: float32 [2048, 6], P(('dp', 'expert')), may hold values from 0.05 to 0.5
- partner: int32 [2048], P(('dp', 'expert')), may hold values from 0 to 3, as said below
- gate_up_weight: bfloat16 [32, 2, 1536, 5120], P('expert', None, 'dp'), may hold values from -0.078125 to 0.078125
- adapter_down_weight: bfloat16 [32, 8, 1536], P('expert', None, 'dp'), may hold values from -0.15625 to 0.15625
- adapter_up_weight: bfloat16 [32, 8, 5120], P('expert', None, 'dp'), may hold values from -2 to 2
Outputs:
- down_factor_gradient: float32 [32, 8, 1536], P('expert', None, 'dp')
- up_factor_gradient: float32 [32, 8, 5120], P('expert', None, 'dp')
Inputs may be any that keep to these rules, and one draw needn't show every extreme that they name: `chosen_expert_index`: in each aligned block of 4 rows (the tokens of one device) a token names 6 different experts, no expert is named by more than 2 rows, a bound that some block reaches. Tokens are paired within each aligned block of 4 rows: partner holds the index of the other token of the pair within the block, never the token itself, and partner of partner is the token.
All inputs are finite; a program needn't handle non-finite values.
Results may differ from a plain program's by a relative error of at most 0.0039.
Values may be sent and summed in bfloat16 or wider, within the bound.
A program may use at most 64 MiB of HBM per device.

v0:
```python
import math

import jax
import jax.numpy as jnp
from jax import lax
from jax.sharding import PartitionSpec as P

adapter_scale = 2.0
control = 0.5
highest_precision = lax.Precision.HIGHEST


def route_tables(chosen_expert_index, router_gate_weight, experts, capacity):
    tok_count, choices = chosen_expert_index.shape
    picks = (chosen_expert_index[:, :, None] == jnp.arange(experts, dtype=jnp.int32)).astype(
        jnp.int32
    )
    flat = picks.reshape(tok_count * choices, experts)
    before = jnp.cumsum(flat, axis=0) - flat
    slots = jnp.sum(before * flat, axis=1).reshape(tok_count, choices)
    places = (slots[:, :, None] == jnp.arange(capacity, dtype=jnp.int32)).astype(jnp.float32)
    chosen = picks.astype(jnp.float32)
    select = jnp.einsum("tke,tkc->ect", chosen, places, precision=highest_precision)
    weighted = jnp.einsum(
        "tke,tkc,tk->ect", chosen, places, router_gate_weight, precision=highest_precision
    )
    return (select.astype(jnp.bfloat16), weighted)


def expert_hidden(rows, w_local):
    flat_rows = rows.reshape(-1, rows.shape[-1])
    both = jnp.einsum("gfd,nd->gfn", w_local, flat_rows, preferred_element_type=jnp.float32)
    return (jax.nn.silu(both[0]) * both[1]).astype(jnp.bfloat16)


def body(
    tokens,
    chosen_expert_index,
    router_gate_weight,
    partner,
    gate_up_weight,
    adapter_down_weight,
    adapter_up_weight,
):
    tok_count, width = tokens.shape
    choices = chosen_expert_index.shape[1]
    groups = lax.axis_size("dp")
    experts = lax.axis_size("expert")
    capacity = min(tok_count, max(2, (2 * tok_count * choices + experts - 1) // experts))
    select, weighted = route_tables(chosen_expert_index, router_gate_weight, experts, capacity)
    w_local = gate_up_weight[0]
    down_factor = adapter_down_weight[0]
    up_factor = adapter_up_weight[0]
    slice_width = up_factor.shape[1]
    outgoing = jnp.einsum("ect,td->ecd", select, tokens, preferred_element_type=jnp.float32).astype(
        jnp.bfloat16
    )
    arrived = lax.all_to_all(outgoing[None], "expert", split_axis=1, concat_axis=1, tiled=True)
    hidden_state = expert_hidden(lax.all_gather(arrived, "dp", axis=0, tiled=True), w_local)
    grid = (groups, experts, capacity)
    partial_low = jnp.einsum(
        "fn,rf->nr", hidden_state, down_factor, preferred_element_type=jnp.float32
    )
    narrow_product = lax.psum(partial_low, "dp")
    delta_flat = (
        adapter_scale
        * jnp.einsum(
            "hy,ya->ha", narrow_product, up_factor.astype(jnp.float32), precision=highest_precision
        )
    ).astype(jnp.bfloat16)
    change_rows = delta_flat.reshape(grid + (slice_width,))
    returned = lax.all_to_all(
        lax.all_to_all(change_rows, "dp", split_axis=0, concat_axis=3, tiled=True),
        "expert",
        split_axis=1,
        concat_axis=1,
        tiled=True,
    )
    returned = returned.reshape(experts, capacity, width)
    delta = jnp.einsum(
        "ect,ecd->td", weighted, returned.astype(jnp.float32), precision=highest_precision
    )
    total = tok_count * groups * experts
    mates = jnp.take(tokens, partner, axis=0).astype(jnp.float32)
    direction = tokens.astype(jnp.float32) - mates
    cotangent = 2.0 / math.sqrt(total) * (delta - control * direction)
    cot_rows = jnp.einsum("ect,td->ecd", weighted, cotangent, precision=highest_precision).astype(
        jnp.bfloat16
    )
    sectioned = cot_rows.reshape(1, experts, capacity, groups, slice_width)
    cot_in = lax.all_to_all(
        lax.all_to_all(sectioned, "dp", split_axis=3, concat_axis=0, tiled=True),
        "expert",
        split_axis=1,
        concat_axis=1,
        tiled=True,
    )
    cot_in = cot_in.reshape(-1, slice_width)
    partial_cot = jnp.einsum("nd,rd->nr", cot_in, up_factor, preferred_element_type=jnp.float32)
    cotangent_narrow = lax.psum(partial_cot, "dp")
    up_factor_gradient = adapter_scale * jnp.einsum(
        "nr,nd->rd", narrow_product, cot_in.astype(jnp.float32), precision=highest_precision
    )
    down_factor_gradient = adapter_scale * jnp.einsum(
        "nr,fn->rf", cotangent_narrow, hidden_state.astype(jnp.float32), precision=highest_precision
    )
    return (down_factor_gradient[None], up_factor_gradient[None])


def solution(mesh):
    placed = (
        P(("dp", "expert"), None),
        P(("dp", "expert"), None),
        P(("dp", "expert"), None),
        P(("dp", "expert")),
        P("expert", None, "dp", None),
        P("expert", None, "dp"),
        P("expert", None, "dp"),
    )
    return jax.shard_map(
        body,
        mesh=mesh,
        in_specs=placed,
        out_specs=(P("expert", None, "dp"), P("expert", None, "dp")),
        check_vma=False,
    )
```

profile of v0, /device:TPU:32, one launch (start us, length us, event | category | flops | bytes accessed | tf_op | source)
XLA Modules:
  0.0 497.6 jit_solution(12382590038935310197)
XLA Ops:
  7.2 0.0 copy-start
  7.2 0.0 all-gather.2.cloned.1.call-start
  7.2 0.9 eq.37
  8.1 0.1 fusion.27
  8.2 0.2 select_reduce_fusion
  8.4 0.1 eq.41
  8.5 0.9 fusion.12
  9.4 1.2 fusion
  10.6 0.7 copy.16
  11.3 53.0 %all_to_all.51 = bf16[1,32,2,5120]{3,2,0,1:T(2,128)(2,1)S(1)} all-to-all(bf16[1,32,2,5120]{3,2,0,1:T(2,128)(2,1)S(1)} %copy.16), channel_id=1, replica_groups=mesh['dp'=16,'expert'=32] {'expert'}, dimensions={1} | all-to-all | bytes 1310720 | tf_op jit(solution)/shard_map/all_to_all | solution.py:58
  64.3 1.0 copy.17
  65.3 0.0 all-gather.2.cloned.1.call-update
  65.3 88.7 %all-gather.2.cloned.1.call-done = bf16[16,32,2,5120]{3,1,2,0:T(8,128)(2,1)} async-done(((bf16[1,32,2,5120]{3,1,2,0:T(8,128)(2,1)}), bf16[16,32,2,5120]{3,1,2,0:T(8,128)(2,1)}) %all-gather.2.cloned.1.call-update) | async-done | bytes 10485776 | tf_op jit(solution)/shard_map/all_gather | solution.py:59
  154.0 20.0 %copy.18 = bf16[16,32,2,5120]{3,2,1,0:T(2,128)(2,1)} copy(bf16[16,32,2,5120]{3,1,2,0:T(8,128)(2,1)} %all-gather.2.cloned.1.call-done) | data formatting | bytes 20971520 | tf_op jit(solution)/shard_map/all_gather | solution.py:59
  173.9 21.2 %reshape.45 = bf16[1024,5120,1]{1,0,2:T(8,128)(2,1)} reshape(bf16[16,32,2,5120]{3,2,1,0:T(2,128)(2,1)} %copy.18) | data formatting | bytes 20971520 | tf_op jit(solution)/shard_map/reshape | solution.py:31
  195.1 0.0 copy-done
  195.1 0.0 copy-start.5
  195.1 7.6 %fusion.7 = f32[2,96,1024]{2,1,0:T(8,128)S(1)} fusion(bf16[1024,5120,1]{1,0,2:T(8,128)(2,1)} %reshape.45, bf16[1,2,96,5120]{3,2,1,0:T(8,128)(2,1)S(1)} %copy-done), kind=kOutput, calls=%fused_computation.12 | convolution fusion | flops 2013265920 | bytes 13238272 | tf_op jit(solution)/shard_map/gfd,nd->gfn/dot_general | solution.py:32
  202.7 0.0 copy-start.8
  202.7 0.9 copy-done.8
  203.6 0.0 copy-done.5
  203.6 0.0 copy-start.3
  203.6 0.2 fusion.19
  203.8 73.0 %psum.14 = f32[1024,8]{0,1:T(8,128)S(1)} all-reduce(f32[1024,8]{0,1:T(8,128)S(1)} %fusion.19), channel_id=1, replica_groups=mesh['dp'=16,'expert'=32] {'dp'}, use_global_device_ids=true, to_apply=%region_2.3 | all-reduce | flops 8192 | bytes 65536 | tf_op jit(solution)/shard_map/psum | solution.py:64
  276.8 0.0 copy-done.3
  276.8 0.0 copy-start.2
  276.8 0.7 fusion.6
  277.5 0.0 copy-done.2
  277.5 0.4 copy.19
  277.9 0.3 reshape.31
  278.3 14.1 %all_to_all.52 = bf16[16,32,2,320]{3,2,1,0:T(2,128)(2,1)S(1)} all-to-all(bf16[16,32,2,320]{3,2,1,0:T(2,128)(2,1)S(1)} %reshape.31), channel_id=1, replica_groups=mesh['dp'=16,'expert'=32] {'dp'}, dimensions={0} | all-to-all | bytes 1310720 | tf_op jit(solution)/shard_map/all_to_all | solution.py:73
  292.4 0.0 copy-start.7
  292.4 0.0 copy-start.1
  292.4 0.0 copy-start.4
  292.4 0.0 copy-start.6
  292.4 0.7 copy.28
  293.2 1.7 reshape.49
  294.8 12.8 %all-to-all-start.2 = ((bf16[1,32,2,5120]{3,2,0,1:T(2,128)(2,1)}), bf16[1,32,2,5120]{3,2,0,1:T(2,128)(2,1)S(1)}, u32[]{:S(2)}, u32[]{:S(2)}) async-start(bf16[1,32,2,5120]{3,2,0,1:T(2,128)(2,1)} %reshape.49), calls=%async_computation.2 | async-start | bytes 1310720 | tf_op jit(solution)/shard_map/all_to_all | solution.py:72
  307.7 0.0 copy-done.7
  307.7 0.0 copy-done.1
  307.7 0.6 gather_fusion
  308.3 0.0 copy-done.4
  308.3 0.0 copy-done.6
  308.3 0.2 convolution_bitcast_fusion.1
  308.6 37.0 %all-to-all-done.2 = bf16[1,32,2,5120]{3,2,0,1:T(2,128)(2,1)S(1)} async-done(((bf16[1,32,2,5120]{3,2,0,1:T(2,128)(2,1)}), bf16[1,32,2,5120]{3,2,0,1:T(2,128)(2,1)S(1)}, u32[]{:S(2)}, u32[]{:S(2)}) %all-to-all-start.2) | async-done | bytes 655392 | tf_op jit(solution)/shard_map/all_to_all | solution.py:72
  345.6 0.4 fusion.3
  346.0 1.3 convolution_convert_fusion
  347.3 0.6 reshape.33
  347.9 0.8 copy.25
  348.7 16.1 %all_to_all.53 = bf16[1,32,2,16,320]{4,2,1,0,3:T(2,128)(2,1)S(1)} all-to-all(bf16[1,32,2,16,320]{4,2,1,0,3:T(2,128)(2,1)S(1)} %copy.25), channel_id=1, replica_groups=mesh['dp'=16,'expert'=32] {'dp'}, dimensions={3} | all-to-all | bytes 1310720 | tf_op jit(solution)/shard_map/all_to_all | solution.py:92
  364.9 0.5 copy.26
  365.4 49.2 %all_to_all.54 = bf16[16,32,2,1,320]{4,2,0,3,1:T(2,128)(2,1)S(1)} all-to-all(bf16[16,32,2,1,320]{4,2,0,3,1:T(2,128)(2,1)S(1)} %copy.26), channel_id=1, replica_groups=mesh['dp'=16,'expert'=32] {'expert'}, dimensions={1} | all-to-all | bytes 1310720 | tf_op jit(solution)/shard_map/all_to_all | solution.py:91
  414.6 0.7 copy.27
  415.3 0.7 reshape.34
  416.0 1.8 fusion.10
  417.7 0.3 fusion.30
  418.0 70.7 %psum.15 = f32[1024,8]{0,1:T(8,128)S(1)} all-reduce(f32[1024,8]{0,1:T(8,128)S(1)} %fusion.30), channel_id=1, replica_groups=mesh['dp'=16,'expert'=32] {'dp'}, use_global_device_ids=true, to_apply=%region_3.4 | all-reduce | flops 8192 | bytes 65536 | tf_op jit(solution)/shard_map/psum | solution.py:100
  488.7 2.0 fusion.11
  (4 shorter events, 0.1 us)
Async XLA Ops:
  7.2 188.0 %copy-start = (bf16[1,2,96,5120]{3,2,1,0:T(8,128)(2,1)S(1)}, bf16[1,2,96,5120]{3,2,1,0:T(8,128)(2,1)}, u32[]{:S(2)}) copy-start(bf16[1,2,96,5120]{3,2,1,0:T(8,128)(2,1)} %param.11) | copy-start | bytes 5898244
  7.2 146.8 %all-gather.2.cloned.1.call-start = ((), (), s32[]{:S(2)}) async-start(), calls=%async_computation.5 | async-start | bytes 11141120 | tf_op jit(solution)/shard_map/all_gather | solution.py:59
  195.1 8.5 %copy-start.5 = (bf16[1,8,96]{2,1,0:T(8,128)(2,1)S(1)}, bf16[1,8,96]{2,1,0:T(8,128)(2,1)}, u32[]{:S(2)}) copy-start(bf16[1,8,96]{2,1,0:T(8,128)(2,1)} %param.12) | copy-start | bytes 4612
  202.7 0.9 copy-start.8
  203.6 73.2 %copy-start.3 = (bf16[1,8,320]{2,1,0:T(8,128)(2,1)S(1)}, bf16[1,8,320]{2,1,0:T(8,128)(2,1)}, u32[]{:S(2)}) copy-start(bf16[1,8,320]{2,1,0:T(8,128)(2,1)} %param.13) | copy-start | bytes 15364
  276.8 0.7 copy-start.2
  292.4 15.3 %copy-start.7 = (s32[4]{0:T(128)S(1)}, s32[4]{0:T(128)}, u32[]{:S(2)}) copy-start(s32[4]{0:T(128)} %param.10) | copy-start | bytes 52
  292.4 15.3 %copy-start.1 = (bf16[4,5120]{1,0:T(4,128)(2,1)S(1)}, bf16[4,5120]{1,0:T(4,128)(2,1)}, u32[]{:S(2)}) copy-start(bf16[4,5120]{1,0:T(4,128)(2,1)} %param.7) | copy-start | bytes 122884
  292.4 15.9 %copy-start.4 = (s32[4,6]{1,0:T(4,128)S(1)}, s32[4,6]{1,0:T(4,128)}, u32[]{:S(2)}) copy-start(s32[4,6]{1,0:T(4,128)} %param.8) | copy-start | bytes 292
  292.4 15.9 %copy-start.6 = (f32[4,6]{1,0:T(4,128)S(1)}, f32[4,6]{1,0:T(4,128)}, u32[]{:S(2)}) copy-start(f32[4,6]{1,0:T(4,128)} %param.9) | copy-start | bytes 292
  294.8 50.7 %all-to-all-start.2 = ((bf16[1,32,2,5120]{3,2,0,1:T(2,128)(2,1)}), bf16[1,32,2,5120]{3,2,0,1:T(2,128)(2,1)S(1)}, u32[]{:S(2)}, u32[]{:S(2)}) async-start(bf16[1,32,2,5120]{3,2,0,1:T(2,128)(2,1)} %reshape.49), calls=%async_computation.2 | async-start | bytes 1310720 | tf_op jit(solution)/shard_map/all_to_all | solution.py:72
Sparse Core Ops, SparseCore 0:
  65.4 88.4 all-gather.1
where the time goes:
time: 499 us; the launch traced here: 498 us
  blocking collectives  276 us (55%)
  waiting for transfers between devices  126 us (25%)
  local copies, waits for them, and re-layouts  51.8 us (10%)
  matrix products  16.6 us (3%)
  between operations  14.2 us (3%)
  starting transfers between devices  12.9 us (3%)
    all_gather x1, waiting for transfers between devices, body(): lax.all_gather(arrived, 'dp', axis=0, tiled=True)  88.7 us
    psum x1, blocking collectives, body(): narrow_product = lax.psum(partial_low, 'dp')  73 us
    psum x1, blocking collectives, body(): cotangent_narrow = lax.psum(partial_cot, 'dp')  70.7 us
    all_to_all x1, blocking collectives, body(): lax.all_to_all(outgoing[None], 'expert', split_axis=1, concat_axis=1, til...  53 us
    all_to_all x1, blocking collectives, body(): lax.all_to_all(lax.all_to_all(sectioned, 'dp', split_axis=3, concat_axis=...  49.2 us
    all_to_all x1, waiting for transfers between devices, body(): lax.all_to_all(lax.all_to_all(change_rows, 'dp', split_axis=0, concat_axi...  37 us
    reshape x1, local copies, waits for them, and re-layouts, expert_hidden(): flat_rows = rows.reshape(-1, rows.shape[-1])  21.2 us
    all_gather x1, local copies, waits for them, and re-layouts, body(): lax.all_gather(arrived, 'dp', axis=0, tiled=True)  20 us
  transfers between devices with their start and end apart: 2, of which 2 were waited for; matrix products, arithmetic and copies ran while one was open for 0% of the time, Pallas kernels for 0%

commit v1 on v0

v1 whole, which is shorter than its diff:
```python
import functools
import math

import jax
import jax.numpy as jnp
from jax import lax
from jax.experimental import pallas as pl
from jax.experimental.pallas import tpu as pltpu
from jax.sharding import PartitionSpec as P

SCALE = 2.0
CONTROL = 0.5
SIDE = 4
HIGH = lax.Precision.HIGHEST
MESH = pl.DeviceIdType.MESH
F32 = jnp.float32
BF16 = jnp.bfloat16


def dot_t(a, b, **kw):
    return lax.dot_general(a, b, (((1,), (1,)), ((), ())), preferred_element_type=F32, **kw)


def split(v):
    hi = v.astype(BF16)
    lo = (v - hi.astype(F32)).astype(BF16)
    return hi, lo


def gather_kernel(
    zs, x_ref, w_ref, b_ref, hid_ref, xs_ref, low_ref,
    xall, wbuf, accg, accu, lowp, lowr, lowz,
    ssem, rsem, lsem, wssem, wrsem, psend, precv, zsend, zrecv,
):
    d_half = x_ref.shape[1] // 2
    quarter = d_half // 2
    units = w_ref.shape[1]
    dp = lax.axis_index("dp")
    ex = lax.axis_index("expert")
    y, x = dp // SIDE, lax.rem(dp, SIDE)
    z, c = ex // 2, lax.rem(ex, 2)
    other = 2 * z + (1 - c)
    groups = SIDE * SIDE

    barrier = pltpu.get_barrier_semaphore()

    def greet_dp(k, carry):
        pl.semaphore_signal(barrier, inc=1, device_id={"dp": lax.rem(dp + k, groups)}, device_id_type=MESH)
        return carry

    def greet_z(k, carry):
        pl.semaphore_signal(
            barrier, inc=1, device_id={"expert": 2 * lax.rem(z + k, zs) + c}, device_id_type=MESH
        )
        return carry

    pl.semaphore_signal(barrier, inc=1, device_id={"expert": other}, device_id_type=MESH)
    lax.fori_loop(1, groups, greet_dp, 0)
    lax.fori_loop(1, zs, greet_z, 0)
    pl.semaphore_wait(barrier, groups + zs - 1)

    def far(h, first, step):
        along_x = (h == 0) == first
        yy = y if along_x else lax.rem(y + step + SIDE, SIDE)
        xx = lax.rem(x + step + SIDE, SIDE) if along_x else x
        return {"dp": yy * SIDE + xx}

    def place(h, da, db):
        dx, dy = (da, db) if h == 0 else (db, da)
        return lax.rem(y + dy + SIDE, SIDE), lax.rem(x + dx + SIDE, SIDE)

    def cols(h, part):
        lo = h * d_half
        if part is None:
            return pl.ds(lo, d_half)
        return pl.ds(lo + part * quarter, quarter)

    started = []

    def send(h, da, db, part, first, step, number):
        by, bx = place(h, da, db)
        block = xall.at[by, bx, :, cols(h, part)]
        source = x_ref.at[:, cols(h, part)] if da == 0 and db == 0 else block
        copy = pltpu.make_async_remote_copy(
            src_ref=source, dst_ref=block, send_sem=ssem.at[number], recv_sem=rsem.at[number],
            device_id=far(h, first, step), device_id_type=MESH,
        )
        copy.start()
        started.append(copy)

    def arrived(h, da, db, part, number):
        by, bx = place(h, da, db)
        block = xall.at[by, bx, :, cols(h, part)]
        pltpu.make_async_remote_copy(
            src_ref=block, dst_ref=block, send_sem=ssem.at[number], recv_sem=rsem.at[number],
            device_id=far(h, True, 1), device_id_type=MESH,
        ).wait_recv()

    offsets = (0, -1, 1, 2)

    def number(h, phase, j, kind):
        return h * 20 + (kind if phase == 0 else 4 + 4 * j + kind)

    own = pltpu.make_async_copy(x_ref, xall.at[y, x], lsem.at[0])
    own.start()
    for h in range(2):
        send(h, 0, 0, None, True, 1, number(h, 0, 0, 0))
        send(h, 0, 0, None, True, -1, number(h, 0, 0, 1))
    weights = []
    for g in range(2):
        mine = pltpu.make_async_copy(w_ref.at[g], wbuf.at[g, pl.ds(0, units)], lsem.at[1 + g])
        mine.start()
        theirs = pltpu.make_async_remote_copy(
            src_ref=w_ref.at[g], dst_ref=wbuf.at[g, pl.ds(units, units)],
            send_sem=wssem.at[g], recv_sem=wrsem.at[g],
            device_id={"expert": other}, device_id_type=MESH,
        )
        theirs.start()
        weights += [mine, theirs]
    for h in range(2):
        send(h, 0, 0, None, False, 1, number(h, 1, 0, 0))
        send(h, 0, 0, None, False, -1, number(h, 1, 0, 1))
    accg[...] = jnp.zeros_like(accg)
    accu[...] = jnp.zeros_like(accu)
    for h in range(2):
        arrived(h, -1, 0, None, number(h, 0, 0, 0))
        send(h, -1, 0, 0, True, 1, number(h, 0, 0, 2))
        arrived(h, 1, 0, None, number(h, 0, 0, 1))
        send(h, 1, 0, 1, True, -1, number(h, 0, 0, 3))
        for j in (1, 2):
            send(h, offsets[j], 0, None, False, 1, number(h, 1, j, 0))
            send(h, offsets[j], 0, None, False, -1, number(h, 1, j, 1))
    for h in range(2):
        arrived(h, 2, 0, 0, number(h, 0, 0, 2))
        arrived(h, 2, 0, 1, number(h, 0, 0, 3))
        send(h, 2, 0, None, False, 1, number(h, 1, 3, 0))
        send(h, 2, 0, None, False, -1, number(h, 1, 3, 1))

    own.wait()
    for copy in weights:
        copy.wait()
    chunk = 512 if d_half % 512 == 0 else d_half
    rows = SIDE * x_ref.shape[0]

    def multiply(h, db):
        by, bx = place(h, 0, db)

        def step(i, carry):
            at = pl.ds(pl.multiple_of(h * d_half + i * chunk, 128), chunk)
            if h == 0:
                block = xall[by, :, :, at]
            else:
                block = xall[:, bx, :, at]
            block = block.reshape(rows, chunk)
            for g, acc in ((0, accg), (1, accu)):
                part = dot_t(block, wbuf[g, :, at]).reshape(SIDE, rows // SIDE, 2 * units)
                if h == 0:
                    acc[by] = acc[by] + part
                else:
                    acc[:, bx] = acc[:, bx] + part
            return carry

        lax.fori_loop(0, d_half // chunk, step, 0)

    for j in range(4):
        for h in range(2):
            arrived(h, offsets[j], -1, None, number(h, 1, j, 0))
            send(h, offsets[j], -1, 0, False, 1, number(h, 1, j, 2))
            arrived(h, offsets[j], 1, None, number(h, 1, j, 1))
            send(h, offsets[j], 1, 1, False, -1, number(h, 1, j, 3))
        if j == 1:
            for h in range(2):
                multiply(h, 0)
    for h in range(2):
        multiply(h, -1)
        multiply(h, 1)
    for h in range(2):
        for j in range(4):
            arrived(h, offsets[j], 2, 0, number(h, 1, j, 2))
            arrived(h, offsets[j], 2, 1, number(h, 1, j, 3))
        multiply(h, 2)

    pair = xs_ref.shape[-1]
    piece = pltpu.make_async_copy(
        xall.at[:, :, :, pl.ds(pl.multiple_of(pair * (dp // 2), 128), pair)], xs_ref, lsem.at[3]
    )
    piece.start()
    tokens = accg.shape[2]
    both = accg.shape[3]
    gate = accg[...].reshape(groups * tokens, both)
    hidden = (gate * (1.0 / (1.0 + jnp.exp(-gate))) * accu[...].reshape(groups * tokens, both)).astype(BF16)
    hid_ref[...] = hidden
    low = dot_t(b_ref[...], hidden)
    for k in range(groups):
        lowp[k, :, 0:tokens] = low[:, k * tokens : (k + 1) * tokens]

    def low_copy(k):
        peer = lax.rem(dp + k, groups)
        return pltpu.make_async_remote_copy(
            src_ref=lowp.at[peer], dst_ref=lowr.at[k], send_sem=psend.at[k], recv_sem=precv.at[k],
            device_id={"dp": peer}, device_id_type=MESH,
        )

    def start_low(k, carry):
        low_copy(k).start()
        return carry

    def wait_low(k, total):
        low_copy(k).wait()
        return total + lowr[k]

    lax.fori_loop(1, groups, start_low, 0)
    total = lax.fori_loop(1, groups, wait_low, lowp[dp])
    lowz[z] = total

    def z_copy(k):
        return pltpu.make_async_remote_copy(
            src_ref=lowz.at[z], dst_ref=lowz.at[z], send_sem=zsend.at[k], recv_sem=zrecv.at[k],
            device_id={"expert": 2 * lax.rem(z + k, zs) + c}, device_id_type=MESH,
        )

    def z_arrival(k):
        source = lax.rem(z - k + zs, zs)
        return pltpu.make_async_remote_copy(
            src_ref=lowz.at[source], dst_ref=lowz.at[source], send_sem=zsend.at[k], recv_sem=zrecv.at[k],
            device_id={"expert": 2 * source + c}, device_id_type=MESH,
        )

    def start_z(k, carry):
        z_copy(k).start()
        return carry

    def wait_z(k, carry):
        z_arrival(k).wait_recv()
        return carry

    def done_z(k, carry):
        z_copy(k).wait_send()
        return carry

    lax.fori_loop(1, zs, start_z, 0)
    lax.fori_loop(1, zs, wait_z, 0)
    low_ref[...] = lowz[...].reshape(low_ref.shape)
    lax.fori_loop(1, zs, done_z, 0)
    for copy in started:
        copy.wait_send()
    piece.wait()


def finish_kernel(
    zs, total, low_ref, w8_ref, q_ref, g_ref, zt_ref, hid_ref, xs_ref, asl_ref, down_ref, up_ref,
    ct, msgs, arrived, cot, chat, half, taken, psend, precv, csend, crecv,
):
    dp = lax.axis_index("dp")
    ex = lax.axis_index("expert")
    z, c = ex // 2, lax.rem(ex, 2)
    other = 2 * z + (1 - c)
    groups = SIDE * SIDE
    tokens = q_ref.shape[0]
    units = down_ref.shape[1]
    width = up_ref.shape[1]
    wide = zs * 16
    factor = 2.0 / math.sqrt(total)

    barrier = pltpu.get_barrier_semaphore()

    def greet(k, carry):
        pl.semaphore_signal(barrier, inc=1, device_id={"dp": lax.rem(dp + k, groups)}, device_id_type=MESH)
        return carry

    pl.semaphore_signal(barrier, inc=1, device_id={"expert": other}, device_id_type=MESH)
    lax.fori_loop(1, groups, greet, 0)

    values = low_ref[:, 0:tokens] * w8_ref[...]
    ct[...] = values
    here = pl.ds(pl.multiple_of(16 * z, 16), 16)
    mine = ct[here, :]
    weight = w8_ref[here, :]
    inner = jnp.dot(g_ref[...], values, precision=HIGH, preferred_element_type=F32)
    msgs[:, 0:tokens] = weight * (factor * (SCALE * inner - CONTROL * zt_ref[...]))
    msgs[:, tokens : 2 * tokens] = jnp.dot(mine, q_ref[...], precision=HIGH, preferred_element_type=F32)
    msgs[:, 2 * tokens : 2 * tokens + wide] = dot_t(mine, values, precision=HIGH)
    arrived[0] = msgs[...]

    pl.semaphore_wait(barrier, groups)

    def copy_of(k):
        return pltpu.make_async_remote_copy(
            src_ref=msgs, dst_ref=arrived.at[k], send_sem=psend.at[k], recv_sem=precv.at[k],
            device_id={"dp": lax.rem(dp + k, groups)}, device_id_type=MESH,
        )

    def start(k, carry):
        copy_of(k).start()
        return carry

    def wait(k, carry):
        copy_of(k).wait()
        return carry

    lax.fori_loop(1, groups, start, 0)
    lax.fori_loop(1, groups, wait, 0)

    gram = arrived[0, :, 2 * tokens : 2 * tokens + wide]
    for k in range(1, groups):
        gram = gram + arrived[k, :, 2 * tokens : 2 * tokens + wide]
    for k in range(groups):
        source = lax.rem(dp - k + groups, groups)
        block = arrived[lax.rem(dp - k + groups, groups)]
        cot[:, k * tokens : (k + 1) * tokens] = block[:, 0:tokens]
        chat[:, k * tokens : (k + 1) * tokens] = block[:, tokens : 2 * tokens]
        del source

    hi, lo = split(cot[...])
    down = jnp.dot(hi, hid_ref[...], preferred_element_type=F32) + jnp.dot(
        lo, hid_ref[...], preferred_element_type=F32
    )
    hi, lo = split(chat[...])
    along = jnp.dot(hi, xs_ref[...], preferred_element_type=F32) + jnp.dot(
        lo, xs_ref[...], preferred_element_type=F32
    )
    along = jnp.where(lax.rem(dp, 2) == 0, along[:, 0:width], along[:, width : 2 * width])
    hi, lo = split(gram)
    through = jnp.dot(hi, asl_ref[...], preferred_element_type=F32) + jnp.dot(
        lo, asl_ref[...], preferred_element_type=F32
    )
    up = (SCALE * factor) * (SCALE * through - CONTROL * along)
    down = SCALE * down
    half[:, 0:units] = down[8:16, units : 2 * units]
    half[:, 128 : 128 + width] = up[8:16, :]
    swap = pltpu.make_async_remote_copy(
        src_ref=half, dst_ref=taken, send_sem=csend, recv_sem=crecv,
        device_id={"expert": other}, device_id_type=MESH,
    )
    swap.start()
    swap.wait()
    down_ref[...] = down[0:8, 0:units] + taken[:, 0:units]
    up_ref[...] = up[0:8, :] + taken[:, 128 : 128 + width]


def whole(space=pltpu.VMEM):
    return pl.BlockSpec(memory_space=space)


def body(tokens, chosen, router, partner, gate_up, a_down, a_up):
    count, d_model = tokens.shape
    groups = lax.axis_size("dp")
    experts = lax.axis_size("expert")
    zs = experts // 2
    units = gate_up.shape[2]
    width = a_up.shape[2]
    ex = lax.axis_index("expert")
    z, c = ex // 2, ex % 2
    rank = a_up.shape[1]
    gtok = zs * count

    relative = jnp.bitwise_xor(chosen, c)
    wtab = jnp.sum(
        jnp.where(relative[:, :, None] == jnp.arange(experts, dtype=jnp.int32), router[:, :, None], 0.0), axis=1
    )
    hi = wtab.astype(BF16)
    mid = (wtab - hi.astype(F32)).astype(BF16)
    low = (wtab - hi.astype(F32) - mid.astype(F32)).astype(BF16)
    mates = (partner[:, None] == jnp.arange(count, dtype=jnp.int32)).astype(BF16)
    pad = 128 - (3 * experts + count) % 128
    sent = jnp.concatenate([tokens, hi, mid, low, mates, jnp.zeros((count, pad), BF16)], axis=1)
    same = [[2 * i + k for i in range(zs)] for k in range(2)]
    held = lax.all_gather(sent, "expert", axis=0, axis_index_groups=same, tiled=True)
    x_group = held[:, :d_model]
    table = held[:, d_model:].astype(F32)
    wgroup = (
        table[:, :experts] + table[:, experts : 2 * experts] + table[:, 2 * experts : 3 * experts]
    )
    w8 = jnp.repeat(wgroup.T, rank, axis=0)
    onehot = table[:, 3 * experts : 3 * experts + count]
    tid = jnp.arange(gtok, dtype=jnp.int32)
    mate_of = jnp.where(
        tid[:, None] // count == tid[None, :] // count, jnp.tile(onehot, (1, zs)), 0.0
    )
    q = jnp.eye(gtok, dtype=F32) - mate_of.T

    packed = jnp.concatenate([a_up[0], a_down[0]], axis=1)
    pairs = lax.all_gather(packed, "expert", axis=0, tiled=False).reshape(zs, 2, rank, width + units)
    pairs = jnp.where(c == 0, pairs, pairs[:, ::-1])
    a_slice = pairs[..., :width].reshape(experts * rank, width)
    here = lax.dynamic_index_in_dim(pairs, z, 0, keepdims=False)
    a_pair = here[..., :width].reshape(2 * rank, width)
    blank = jnp.zeros((rank, units), BF16)
    b_pair = jnp.concatenate(
        [
            jnp.concatenate([a_down[0], blank], axis=1),
            jnp.concatenate([blank, here[1, :, width:]], axis=1),
        ],
        axis=0,
    )
    part = dot_t(a_pair, a_slice)
    summed = lax.all_gather(jnp.concatenate([a_pair.astype(F32), part], axis=1), "dp", axis=0, tiled=False)
    g16 = jnp.sum(summed[:, :, width:], axis=0)
    a_full = summed[:, :, :width].astype(BF16).transpose(1, 0, 2).reshape(2 * rank, groups * width)

    hidden, xs, lows = pl.pallas_call(
        functools.partial(gather_kernel, zs),
        out_shape=(
            jax.ShapeDtypeStruct((groups * gtok, 2 * units), BF16),
            jax.ShapeDtypeStruct((SIDE, SIDE, gtok, 2 * width), BF16),
            jax.ShapeDtypeStruct((zs * 16, 128), F32),
        ),
        in_specs=[whole(), whole(pl.ANY), whole()],
        out_specs=(whole(), whole(pl.ANY), whole()),
        scratch_shapes=[
            pltpu.VMEM((SIDE, SIDE, gtok, d_model), BF16),
            pltpu.VMEM((2, 2 * units, d_model), BF16),
            pltpu.VMEM((SIDE, SIDE, gtok, 2 * units), F32),
            pltpu.VMEM((SIDE, SIDE, gtok, 2 * units), F32),
            pltpu.VMEM((groups, 16, 128), F32),
            pltpu.VMEM((groups, 16, 128), F32),
            pltpu.VMEM((zs, 16, 128), F32),
            pltpu.SemaphoreType.DMA((40,)),
            pltpu.SemaphoreType.DMA((40,)),
            pltpu.SemaphoreType.DMA((4,)),
            pltpu.SemaphoreType.DMA((2,)),
            pltpu.SemaphoreType.DMA((2,)),
            pltpu.SemaphoreType.DMA((groups,)),
            pltpu.SemaphoreType.DMA((groups,)),
            pltpu.SemaphoreType.DMA((zs,)),
            pltpu.SemaphoreType.DMA((zs,)),
        ],
        compiler_params=pltpu.CompilerParams(
            collective_id=0, has_side_effects=True, vmem_limit_bytes=48 << 20
        ),
        name="gather_low",
    )(x_group, gate_up[0], b_pair)

    tall = dot_t(a_full, x_group)
    zt = jnp.dot(tall, q, precision=HIGH)

    mw = 2 * gtok + max(128, zs * 16)
    total = count * groups * experts
    down, up = pl.pallas_call(
        functools.partial(finish_kernel, zs, total),
        out_shape=(
            jax.ShapeDtypeStruct((rank, units), F32),
            jax.ShapeDtypeStruct((rank, width), F32),
        ),
        in_specs=[whole()] * 8,
        out_specs=(whole(), whole()),
        scratch_shapes=[
            pltpu.VMEM((zs * 16, gtok), F32),
            pltpu.VMEM((16, mw), F32),
            pltpu.VMEM((groups, 16, mw), F32),
            pltpu.VMEM((16, groups * gtok), F32),
            pltpu.VMEM((16, groups * gtok), F32),
            pltpu.VMEM((8, 128 + width), F32),
            pltpu.VMEM((8, 128 + width), F32),
            pltpu.SemaphoreType.DMA((groups,)),
            pltpu.SemaphoreType.DMA((groups,)),
            pltpu.SemaphoreType.DMA,
            pltpu.SemaphoreType.DMA,
        ],
        compiler_params=pltpu.CompilerParams(
            collective_id=1, has_side_effects=True, vmem_limit_bytes=32 << 20
        ),
        name="finish",
    )(lows, w8, q, g16, zt, hidden, xs.reshape(groups * gtok, 2 * width), a_slice)
    return (down[None], up[None])


def solution(mesh):
    placed = (
        P(("dp", "expert"), None),
        P(("dp", "expert"), None),
        P(("dp", "expert"), None),
        P(("dp", "expert")),
        P("expert", None, "dp", None),
        P("expert", None, "dp"),
        P("expert", None, "dp"),
    )
    return jax.shard_map(
        body,
        mesh=mesh,
        in_specs=placed,
        out_specs=(P("expert", None, "dp"), P("expert", None, "dp")),
        check_vma=False,
    )
```

time: 499 us -> 195 us (0.39)
  the two profiles are of different devices: /device:TPU:32 before, /device:TPU:1 now
where the time goes in v1:
time: 195 us
  Pallas kernels  100 us (51%)
  blocking collectives  83.3 us (43%)
  local copies, waits for them, and re-layouts  5.26 us (3%)
  other arithmetic  4.78 us (2%)
    pallas_call x1, Pallas kernels, body(): pl.pallas_call(functools.partial(gather_kernel, zs), out_shape=(jax.Shape...  80.8 us
    all_gather x1, blocking collectives, body(): lax.all_gather(packed, 'expert', axis=0, tiled=False)  38.3 us
    all_gather x1, blocking collectives, body(): lax.all_gather(sent, 'expert', axis=0, axis_index_groups=same, tiled=True)  25.9 us
    all_gather x1, blocking collectives, body(): lax.all_gather(jnp.concatenate([a_pair.astype(F32), part], axis=1), 'dp',...  19.2 us
    pallas_call x1, Pallas kernels, body(): pl.pallas_call(functools.partial(finish_kernel, zs, total), out_shape=(ja...  19.2 us

profile of v1, /device:TPU:1, one launch (start us, length us, event | category | flops | bytes accessed | tf_op | source)
XLA Modules:
  0.0 194.7 jit_solution(6326280780022978616)
XLA Ops:
  0.7 0.5 and_select_fusion
  1.2 0.7 fusion.7
  1.9 0.7 broadcast_xor_fusion
  2.6 0.1 copy.19
  2.7 0.8 copy.20
  3.4 0.1 select_reduce_fusion
  3.5 0.8 pad_maximum_fusion.1
  4.3 0.9 concatenate.18
  5.2 38.3 %all-gather = bf16[256,416]{1,0:T(8,128)(2,1)S(1)} all-gather(bf16[8,416]{1,0:T(8,128)(2,1)S(1)} %pad_maximum_fusion.1), channel_id=2, replica_groups=mesh['dp'=16,'expert'=32] {'expert'}, dimensions={0}, use_global_device_ids=true | all-gather | bytes 219648 | tf_op jit(solution)/shard_map/all_gather | solution.py:383
  43.5 0.1 reverse_select_fusion
  43.6 0.1 slice_bitcast_fusion.2
  43.7 0.8 fusion.6.b_ref
  44.4 0.1 fusion.4
  44.6 0.1 pad_maximum_fusion
  44.7 19.2 %all-gather.1 = f32[256,576]{1,0:T(8,128)S(1)} all-gather(f32[16,576]{1,0:T(8,128)S(1)} %pad_maximum_fusion), channel_id=3, replica_groups=mesh['dp'=16,'expert'=32] {'dp'}, dimensions={0}, use_global_device_ids=true | all-gather | bytes 626688 | tf_op jit(solution)/shard_map/all_gather | solution.py:397
  63.9 0.1 slice_reduce_fusion.g_ref
  64.1 0.2 reshape.107
  64.3 25.9 %all-gather.2 = bf16[16,4,5248]{2,1,0:T(4,128)(2,1)} all-gather(bf16[1,4,5248]{2,1,0:T(4,128)(2,1)S(1)} %bitcast.41), channel_id=1, replica_groups={{0,2,4,6,8,10,12,14,16,18,20,22,24,26,28,30},{1,3,5,7,9,11,13,15,17,19,..., dimensions={0}, use_global_device_ids=true | all-gather | bytes 713728 | tf_op jit(solution)/shard_map/all_gather | solution.py:368
  90.2 0.0 copy-start
  90.2 1.7 reshape.113
  91.8 0.3 fusion.9
  92.1 0.1 slice.45.x_ref
  92.2 0.1 slice.51
  92.3 0.1 copy.22
  92.3 0.1 fusion.1
  92.4 0.1 copy.21
  92.5 0.8 bitcast_subtract_fusion.q_ref
  93.3 0.1 fusion.11.zt_ref
  93.5 0.0 copy-done
  93.5 80.8 %gather_low.1 = (bf16[1024,192]{1,0:T(8,128)(2,1)S(1)}, bf16[4,4,64,640]{3,2,1,0:T(8,128)(2,1)S(1)}, f32[256,128]{1,0:T(8,128)S(1)}) custom-call(bf16[64,5120]{1,0:T(8,128)(2,1)S(1)} %slice.45.x_ref, bf16[2,96,5120]{2,1,0:T(8,128)(2,1)S(1)} %bitcast.32, bf16[16,192]{1,0:T(8,128)(2,1)S(1)} %fusion.6.b_ref), custom_call_target="tpu_custom_call" | custom-call | tf_op jit(solution)/shard_map/gather_low/pallas_call | solution.py:401
  174.3 19.2 %finish.1 = (f32[8,96]{1,0:T(8,128)S(1)}, f32[8,320]{1,0:T(8,128)S(1)}) custom-call(f32[256,128]{1,0:T(8,128)S(1)} %get-tuple-element.7.low_ref, f32[256,64]{1,0:T(8,128)S(1)} %broadcast_bitcast_fusion.w8_ref, f32[64,64]{1,0:T(8,128)S(1)} %bitcast_subtract_fusion.q_ref, f32[16,256]{1,0:T(8,128)S(1)} %slice_reduce_fusion.g_ref, f32[16,64]{1,0:T(8,128)S(1)} %fusion.11.zt_ref, ...), custom_call_target="tpu_custom_call" | custom-call | tf_op jit(solution)/shard_map/finish/pallas_call | solution.py:439
  193.5 0.6 copy.26
  194.1 0.6 copy.27
  (10 shorter events, 0.2 us)
Async XLA Ops:
  90.2 3.3 %copy-start = (bf16[1,2,96,5120]{3,2,1,0:T(8,128)(2,1)S(1)}, bf16[1,2,96,5120]{3,2,1,0:T(8,128)(2,1)}, u32[]{:S(2)}) copy-start(bf16[1,2,96,5120]{3,2,1,0:T(8,128)(2,1)} %param.11) | copy-start | bytes 5898244

commit v2 on v1

v2 whole, which is shorter than its diff:
```python
import functools
import math

import jax
import jax.numpy as jnp
from jax import lax
from jax.experimental import pallas as pl
from jax.experimental.pallas import tpu as pltpu
from jax.sharding import PartitionSpec as P

SCALE = 2.0
CONTROL = 0.5
SIDE = 4
HIGH = lax.Precision.HIGHEST
MESH = pl.DeviceIdType.MESH
F32 = jnp.float32
BF16 = jnp.bfloat16


def dot_t(a, b, **kw):
    return lax.dot_general(a, b, (((1,), (1,)), ((), ())), preferred_element_type=F32, **kw)


def split(v):
    hi = v.astype(BF16)
    lo = (v - hi.astype(F32)).astype(BF16)
    return hi, lo


def step_kernel(
    zs, total, tok_ref, ids_ref, route_ref, mate_ref, w_ref, adn_ref, aup_ref, down_ref, up_ref,
    zg, xf, xg, tab, pk, pks, apair, apad, aall, bd, gsend, grecv,
    xall, wbuf, accg, accu, hid, lowp, lowr, lowz, ct, msgs, met, cot, chat, half, taken,
    ssem, rsem, lsem, wssem, wrsem, asend, arecv, rsend, rrecv, lsend, lrecv,
    azsend, azrecv, gssem, grsem, psend, precv, zsend, zrecv, msend, mrecv, csend, crecv,
):
    count, d_model = tok_ref.shape
    d_half = d_model // 2
    quarter = d_half // 2
    units = w_ref.shape[1]
    width = aup_ref.shape[1]
    aw = apair.shape[1]
    tokens = zs * count
    experts = 2 * zs
    wide = zs * 16
    factor = 2.0 / math.sqrt(total)
    dp = lax.axis_index("dp")
    ex = lax.axis_index("expert")
    y, x = dp // SIDE, lax.rem(dp, SIDE)
    z, c = ex // 2, lax.rem(ex, 2)
    other = 2 * z + (1 - c)
    groups = SIDE * SIDE

    barrier = pltpu.get_barrier_semaphore()

    def greet_dp(k, carry):
        pl.semaphore_signal(barrier, inc=1, device_id={"dp": lax.rem(dp + k, groups)}, device_id_type=MESH)
        return carry

    def greet_z(k, carry):
        pl.semaphore_signal(
            barrier, inc=1, device_id={"expert": 2 * lax.rem(z + k, zs) + c}, device_id_type=MESH
        )
        return carry

    lax.fori_loop(1, zs, greet_z, 0)
    pl.semaphore_signal(barrier, inc=1, device_id={"expert": other}, device_id_type=MESH)
    lax.fori_loop(1, groups, greet_dp, 0)

    col = lax.broadcasted_iota(jnp.int32, (count, 128), 1)
    named = lax.rem(col, experts)
    wtab = jnp.zeros((count, 128), F32)
    for k in range(ids_ref.shape[1]):
        place_of = jnp.bitwise_xor(ids_ref[:, k : k + 1], c)
        wtab = wtab + jnp.where(named == place_of, route_ref[:, k : k + 1], 0.0)
    top = wtab.astype(BF16).astype(F32)
    mid = (wtab - top).astype(BF16).astype(F32)
    rest = wtab - top - mid
    pick = (col - 3 * experts == mate_ref[...]).astype(F32)
    packed = jnp.where(
        col < experts, top, jnp.where(col < 2 * experts, mid, jnp.where(col < 3 * experts, rest, pick))
    )
    zg[z, :, 0:d_model] = tok_ref[...]
    zg[z, :, d_model : d_model + 128] = packed.astype(BF16)
    pk[...] = jnp.zeros_like(pk)
    pk[:, 0:width] = aup_ref[...]
    pk[:, aw : aw + units] = adn_ref[...]

    pl.semaphore_wait(barrier, groups + zs - 1)

    def line(rightward, s):
        step = 1 if rightward else -1
        block = lax.rem(z - step * s + zs, zs)
        return pltpu.make_async_remote_copy(
            src_ref=zg.at[block], dst_ref=zg.at[block],
            send_sem=(rsend if rightward else lsend).at[s], recv_sem=(rrecv if rightward else lrecv).at[s],
            device_id={"expert": 2 * lax.rem(z + step + zs, zs) + c}, device_id_type=MESH,
        )

    def landed(rightward, s):
        step = 1 if rightward else -1
        block = lax.rem(z - step * (s + 1) + zs, zs)
        pltpu.make_async_remote_copy(
            src_ref=zg.at[block], dst_ref=zg.at[block],
            send_sem=(rsend if rightward else lsend).at[s], recv_sem=(rrecv if rightward else lrecv).at[s],
            device_id={"expert": 2 * lax.rem(z + step + zs, zs) + c}, device_id_type=MESH,
        ).wait_recv()

    reach_r, reach_l = zs // 2, zs - 1 - zs // 2
    line(True, 0).start()
    if reach_l > 0:
        line(False, 0).start()
    swap_a = pltpu.make_async_remote_copy(
        src_ref=pk, dst_ref=pks, send_sem=asend, recv_sem=arecv,
        device_id={"expert": other}, device_id_type=MESH,
    )
    swap_a.start()
    weights = []
    for g in range(2):
        mine = pltpu.make_async_copy(w_ref.at[g], wbuf.at[g, pl.ds(0, units)], lsem.at[1 + g])
        mine.start()
        theirs = pltpu.make_async_remote_copy(
            src_ref=w_ref.at[g], dst_ref=wbuf.at[g, pl.ds(units, units)],
            send_sem=wssem.at[g], recv_sem=wrsem.at[g],
            device_id={"expert": other}, device_id_type=MESH,
        )
        theirs.start()
        weights += [mine, theirs]
    accg[...] = jnp.zeros_like(accg)
    accu[...] = jnp.zeros_like(accu)

    def hop(s, carry):
        landed(True, s - 1)
        line(True, s).start()
        landed(False, s - 1)
        line(False, s).start()
        return carry

    lax.fori_loop(1, min(reach_r, reach_l), hop, 0)
    if reach_l > 0:
        landed(False, reach_l - 1)
    if reach_r > reach_l and reach_r > 1:
        landed(True, reach_r - 2)
        line(True, reach_r - 1).start()
    landed(True, reach_r - 1)

    for k in range(zs):
        xf[count * k : count * (k + 1), :] = zg[k].astype(F32)
    xg[...] = xf[:, 0:d_model].astype(BF16)
    tab[...] = xf[:, d_model : d_model + 128].astype(BF16)

    def far(h, first, step):
        along_x = (h == 0) == first
        yy = y if along_x else lax.rem(y + step + SIDE, SIDE)
        xx = lax.rem(x + step + SIDE, SIDE) if along_x else x
        return {"dp": yy * SIDE + xx}

    def place(h, da, db):
        dx, dy = (da, db) if h == 0 else (db, da)
        return lax.rem(y + dy + SIDE, SIDE), lax.rem(x + dx + SIDE, SIDE)

    def cols(h, part):
        lo = h * d_half
        if part is None:
            return pl.ds(lo, d_half)
        return pl.ds(lo + part * quarter, quarter)

    started = []

    def send(h, da, db, part, first, step, number):
        by, bx = place(h, da, db)
        block = xall.at[by, bx, :, cols(h, part)]
        source = xg.at[:, cols(h, part)] if da == 0 and db == 0 else block
        copy = pltpu.make_async_remote_copy(
            src_ref=source, dst_ref=block, send_sem=ssem.at[number], recv_sem=rsem.at[number],
            device_id=far(h, first, step), device_id_type=MESH,
        )
        copy.start()
        started.append(copy)

    def arrived(h, da, db, part, number):
        by, bx = place(h, da, db)
        block = xall.at[by, bx, :, cols(h, part)]
        pltpu.make_async_remote_copy(
            src_ref=block, dst_ref=block, send_sem=ssem.at[number], recv_sem=rsem.at[number],
            device_id=far(h, True, 1), device_id_type=MESH,
        ).wait_recv()

    offsets = (0, -1, 1, 2)

    def number(h, phase, j, kind):
        return h * 20 + (kind if phase == 0 else 4 + 4 * j + kind)

    for h in range(2):
        send(h, 0, 0, None, True, 1, number(h, 0, 0, 0))
        send(h, 0, 0, None, True, -1, number(h, 0, 0, 1))
    for h in range(2):
        send(h, 0, 0, None, False, 1, number(h, 1, 0, 0))
        send(h, 0, 0, None, False, -1, number(h, 1, 0, 1))
    own = pltpu.make_async_copy(xg, xall.at[y, x], lsem.at[0])
    own.start()

    swap_a.wait()
    lead, follow = pk[...].astype(F32), pks[...].astype(F32)
    stacked = jnp.concatenate([lead, follow], axis=0)
    apair[...] = stacked[:, 0:aw].astype(BF16)
    aall[z] = stacked[:, 0:aw].astype(BF16)
    spread = jnp.concatenate([stacked[:, 0:width], jnp.zeros((16, width), F32)], axis=1)
    odd = jnp.concatenate([jnp.zeros((16, width), F32), stacked[:, 0:width]], axis=1)
    apad[...] = jnp.where(lax.rem(dp, 2) == 0, spread, odd).astype(BF16)
    blank = jnp.zeros((8, units), F32)
    bd[...] = jnp.concatenate(
        [
            jnp.concatenate([lead[:, aw : aw + units], blank], axis=1),
            jnp.concatenate([blank, follow[:, aw : aw + units]], axis=1),
        ],
        axis=0,
    ).astype(BF16)

    def a_copy(k):
        return pltpu.make_async_remote_copy(
            src_ref=apair, dst_ref=aall.at[z], send_sem=azsend.at[k], recv_sem=azrecv.at[k],
            device_id={"expert": 2 * lax.rem(z + k, zs) + c}, device_id_type=MESH,
        )

    def a_arrival(k):
        source = lax.rem(z - k + zs, zs)
        return pltpu.make_async_remote_copy(
            src_ref=apair, dst_ref=aall.at[source], send_sem=azsend.at[k], recv_sem=azrecv.at[k],
            device_id={"expert": 2 * source + c}, device_id_type=MESH,
        )

    def start_a(k, carry):
        a_copy(k).start()
        return carry

    def wait_a(k, carry):
        a_arrival(k).wait_recv()
        a_copy(k).wait_send()
        return carry

    lax.fori_loop(1, zs, start_a, 0)

    for h in range(2):
        arrived(h, -1, 0, None, number(h, 0, 0, 0))
        send(h, -1, 0, 0, True, 1, number(h, 0, 0, 2))
        arrived(h, 1, 0, None, number(h, 0, 0, 1))
        send(h, 1, 0, 1, True, -1, number(h, 0, 0, 3))
        for j in (1, 2):
            send(h, offsets[j], 0, None, False, 1, number(h, 1, j, 0))
            send(h, offsets[j], 0, None, False, -1, number(h, 1, j, 1))
    for h in range(2):
        arrived(h, 2, 0, 0, number(h, 0, 0, 2))
        arrived(h, 2, 0, 1, number(h, 0, 0, 3))
        send(h, 2, 0, None, False, 1, number(h, 1, 3, 0))
        send(h, 2, 0, None, False, -1, number(h, 1, 3, 1))

    own.wait()
    for copy in weights:
        copy.wait()
    chunk = 512 if d_half % 512 == 0 else d_half
    rows = SIDE * tokens

    def multiply(h, db):
        by, bx = place(h, 0, db)

        def step(i, carry):
            at = pl.ds(pl.multiple_of(h * d_half + i * chunk, 128), chunk)
            if h == 0:
                block = xall[by, :, :, at]
            else:
                block = xall[:, bx, :, at]
            block = block.reshape(rows, chunk)
            for g, acc in ((0, accg), (1, accu)):
                part = dot_t(block, wbuf[g, :, at]).reshape(SIDE, rows // SIDE, 2 * units)
                if h == 0:
                    acc[by] = acc[by] + part
                else:
                    acc[:, bx] = acc[:, bx] + part
            return carry

        lax.fori_loop(0, d_half // chunk, step, 0)

    def g_copy(k):
        return pltpu.make_async_remote_copy(
            src_ref=gsend, dst_ref=grecv.at[k], send_sem=gssem.at[k], recv_sem=grsem.at[k],
            device_id={"dp": lax.rem(dp + k, groups)}, device_id_type=MESH,
        )

    def start_g(k, carry):
        g_copy(k).start()
        return carry

    def wait_g(k, carry):
        g_copy(k).wait()
        return carry + grecv[k]

    for j in range(4):
        for h in range(2):
            arrived(h, offsets[j], -1, None, number(h, 1, j, 0))
            send(h, offsets[j], -1, 0, False, 1, number(h, 1, j, 2))
            arrived(h, offsets[j], 1, None, number(h, 1, j, 1))
            send(h, offsets[j], 1, 1, False, -1, number(h, 1, j, 3))
        if j == 0:
            lax.fori_loop(1, zs, wait_a, 0)
            gsend[...] = dot_t(apair[...], aall[...].reshape(wide, aw))
            lax.fori_loop(1, groups, start_g, 0)
        if j == 1:
            for h in range(2):
                multiply(h, 0)
    for h in range(2):
        multiply(h, -1)
        multiply(h, 1)
    gmat = lax.fori_loop(1, groups, wait_g, gsend[...])
    for h in range(2):
        for j in range(4):
            arrived(h, offsets[j], 2, 0, number(h, 1, j, 2))
            arrived(h, offsets[j], 2, 1, number(h, 1, j, 3))
        multiply(h, 2)

    both = accg.shape[3]
    gate = accg[...].reshape(groups * tokens, both)
    hid[...] = (gate * (1.0 / (1.0 + jnp.exp(-gate))) * accu[...].reshape(groups * tokens, both)).astype(BF16)
    strip = pl.ds(pl.multiple_of(2 * width * (dp // 2), 128), 2 * width)
    low = dot_t(bd[...], hid[...])
    tall = dot_t(apad[...], xall[:, :, :, strip].reshape(groups * tokens, 2 * width))
    for k in range(groups):
        lowp[k, :, 0:tokens] = low[:, k * tokens : (k + 1) * tokens]
        lowp[k, :, 64 : 64 + tokens] = tall[:, k * tokens : (k + 1) * tokens]

    def low_copy(k):
        peer = lax.rem(dp + k, groups)
        return pltpu.make_async_remote_copy(
            src_ref=lowp.at[peer], dst_ref=lowr.at[k], send_sem=psend.at[k], recv_sem=precv.at[k],
            device_id={"dp": peer}, device_id_type=MESH,
        )

    def start_low(k, carry):
        low_copy(k).start()
        return carry

    def wait_low(k, carry):
        low_copy(k).wait()
        return carry + lowr[k]

    lax.fori_loop(1, groups, start_low, 0)
    row = lax.broadcasted_iota(jnp.int32, (wide, 128), 0)
    lane = lax.broadcasted_iota(jnp.int32, (wide, 128), 1)
    chooser = jnp.where((row // 8 == lax.rem(lane, experts)) & (lane < 3 * experts), 1.0, 0.0).astype(BF16)
    w8 = dot_t(chooser, tab[...])
    trow = lax.broadcasted_iota(jnp.int32, (tokens, 128), 0)
    tlane = lax.broadcasted_iota(jnp.int32, (tokens, 128), 1)
    finder = jnp.where(tlane - 3 * experts == lax.rem(trow, count), 1.0, 0.0).astype(BF16)
    t0 = lax.broadcasted_iota(jnp.int32, (tokens, tokens), 0)
    t1 = lax.broadcasted_iota(jnp.int32, (tokens, tokens), 1)
    mate = jnp.where(t0 // count == t1 // count, dot_t(finder, tab[...]), 0.0)
    q = jnp.where(t0 == t1, 1.0, 0.0) - mate
    summed = lax.fori_loop(1, groups, wait_low, lowp[dp])
    lowz[z] = summed

    def z_copy(k):
        return pltpu.make_async_remote_copy(
            src_ref=lowz.at[z], dst_ref=lowz.at[z], send_sem=zsend.at[k], recv_sem=zrecv.at[k],
            device_id={"expert": 2 * lax.rem(z + k, zs) + c}, device_id_type=MESH,
        )

    def z_arrival(k):
        source = lax.rem(z - k + zs, zs)
        return pltpu.make_async_remote_copy(
            src_ref=lowz.at[source], dst_ref=lowz.at[source], send_sem=zsend.at[k], recv_sem=zrecv.at[k],
            device_id={"expert": 2 * source + c}, device_id_type=MESH,
        )

    def start_z(k, carry):
        z_copy(k).start()
        return carry

    def wait_z(k, carry):
        z_arrival(k).wait_recv()
        return carry

    def done_z(k, carry):
        z_copy(k).wait_send()
        return carry

    lax.fori_loop(1, zs, start_z, 0)
    zt = jnp.dot(summed[:, 64 : 64 + tokens], q, precision=HIGH, preferred_element_type=F32)
    lax.fori_loop(1, zs, wait_z, 0)

    values = lowz[...].reshape(wide, 128)[:, 0:tokens] * w8
    ct[:, 0:tokens] = values
    ct[:, 64 : 64 + tokens] = w8
    here = pl.ds(pl.multiple_of(16 * z, 16), 16)
    mine = ct[here, 0:tokens]
    weight = ct[here, 64 : 64 + tokens]
    inner = jnp.dot(gmat, values, precision=HIGH, preferred_element_type=F32)
    msgs[:, 0:tokens] = weight * (factor * (SCALE * inner - CONTROL * zt))
    msgs[:, tokens : 2 * tokens] = jnp.dot(mine, q, precision=HIGH, preferred_element_type=F32)
    msgs[:, 2 * tokens : 2 * tokens + wide] = dot_t(mine, values, precision=HIGH)

    def m_copy(k):
        return pltpu.make_async_remote_copy(
            src_ref=msgs, dst_ref=met.at[k], send_sem=msend.at[k], recv_sem=mrecv.at[k],
            device_id={"dp": lax.rem(dp + k, groups)}, device_id_type=MESH,
        )

    def start_m(k, carry):
        m_copy(k).start()
        return carry

    def wait_m(k, carry):
        m_copy(k).wait()
        return carry + met[k, :, 2 * tokens : 2 * tokens + wide]

    lax.fori_loop(1, groups, start_m, 0)
    met[0] = msgs[...]
    lax.fori_loop(1, zs, done_z, 0)

    def done_line(s, carry):
        line(True, s).wait_send()
        return carry

    def done_left(s, carry):
        line(False, s).wait_send()
        return carry

    lax.fori_loop(0, reach_r, done_line, 0)
    lax.fori_loop(0, reach_l, done_left, 0)
    for copy in started:
        copy.wait_send()
    gram = lax.fori_loop(1, groups, wait_m, msgs[:, 2 * tokens : 2 * tokens + wide])
    for k in range(groups):
        block = met[lax.rem(dp - k + groups, groups)]
        cot[:, k * tokens : (k + 1) * tokens] = block[:, 0:tokens]
        chat[:, k * tokens : (k + 1) * tokens] = block[:, tokens : 2 * tokens]

    def both_parts(v, right):
        hi, lo = split(v)
        return jnp.dot(hi, right, preferred_element_type=F32) + jnp.dot(lo, right, preferred_element_type=F32)

    down = SCALE * both_parts(cot[...], hid[...])
    along = both_parts(chat[...], xall[:, :, :, strip].reshape(groups * tokens, 2 * width))
    along = jnp.where(lax.rem(dp, 2) == 0, along[:, 0:width], along[:, width : 2 * width])
    through = both_parts(gram, aall[...].reshape(wide, aw))[:, 0:width]
    up = (SCALE * factor) * (SCALE * through - CONTROL * along)
    half[:, 0:units] = down[8:16, units : 2 * units]
    half[:, 128 : 128 + width] = up[8:16, :]
    swap = pltpu.make_async_remote_copy(
        src_ref=half, dst_ref=taken, send_sem=csend, recv_sem=crecv,
        device_id={"expert": other}, device_id_type=MESH,
    )
    swap.start()
    swap.wait()
    down_ref[...] = down[0:8, 0:units] + taken[:, 0:units]
    up_ref[...] = up[0:8, :] + taken[:, 128 : 128 + width]


def whole(space=pltpu.VMEM):
    return pl.BlockSpec(memory_space=space)


def body(tokens, chosen, router, partner, gate_up, a_down, a_up):
    count, d_model = tokens.shape
    groups = lax.axis_size("dp")
    experts = lax.axis_size("expert")
    zs = experts // 2
    units = gate_up.shape[2]
    width = a_up.shape[2]
    rank = a_up.shape[1]
    gtok = zs * count
    wide = zs * 16
    aw = -(-width // 128) * 128
    mw = 2 * gtok + max(128, wide)
    total = count * groups * experts
    dma = pltpu.SemaphoreType.DMA
    down, up = pl.pallas_call(
        functools.partial(step_kernel, zs, total),
        out_shape=(
            jax.ShapeDtypeStruct((rank, units), F32),
            jax.ShapeDtypeStruct((rank, width), F32),
        ),
        in_specs=[whole()] * 4 + [whole(pl.ANY)] + [whole()] * 2,
        out_specs=(whole(), whole()),
        scratch_shapes=[
            pltpu.VMEM((zs, count, d_model + 128), BF16),
            pltpu.VMEM((gtok, d_model + 128), F32),
            pltpu.VMEM((gtok, d_model), BF16),
            pltpu.VMEM((gtok, 128), BF16),
            pltpu.VMEM((rank, aw + 128), BF16),
            pltpu.VMEM((rank, aw + 128), BF16),
            pltpu.VMEM((16, aw), BF16),
            pltpu.VMEM((16, 2 * width), BF16),
            pltpu.VMEM((zs, 16, aw), BF16),
            pltpu.VMEM((16, 2 * units), BF16),
            pltpu.VMEM((16, wide), F32),
            pltpu.VMEM((groups, 16, wide), F32),
            pltpu.VMEM((SIDE, SIDE, gtok, d_model), BF16),
            pltpu.VMEM((2, 2 * units, d_model), BF16),
            pltpu.VMEM((SIDE, SIDE, gtok, 2 * units), F32),
            pltpu.VMEM((SIDE, SIDE, gtok, 2 * units), F32),
            pltpu.VMEM((groups * gtok, 2 * units), BF16),
            pltpu.VMEM((groups, 16, 128), F32),
            pltpu.VMEM((groups, 16, 128), F32),
            pltpu.VMEM((zs, 16, 128), F32),
            pltpu.VMEM((wide, 128), F32),
            pltpu.VMEM((16, mw), F32),
            pltpu.VMEM((groups, 16, mw), F32),
            pltpu.VMEM((16, groups * gtok), F32),
            pltpu.VMEM((16, groups * gtok), F32),
            pltpu.VMEM((8, 128 + aw), F32),
            pltpu.VMEM((8, 128 + aw), F32),
            dma((40,)), dma((40,)), dma((4,)), dma((2,)), dma((2,)), dma, dma,
            dma((zs,)), dma((zs,)), dma((zs,)), dma((zs,)),
            dma((zs,)), dma((zs,)), dma((groups,)), dma((groups,)), dma((groups,)), dma((groups,)),
            dma((zs,)), dma((zs,)), dma((groups,)), dma((groups,)), dma, dma,
        ],
        compiler_params=pltpu.CompilerParams(
            collective_id=0, has_side_effects=True, vmem_limit_bytes=56 << 20
        ),
        name="lorra_step",
    )(tokens, chosen, router, partner.reshape(count, 1), gate_up[0], a_down[0], a_up[0])
    return (down[None], up[None])


def solution(mesh):
    placed = (
        P(("dp", "expert"), None),
        P(("dp", "expert"), None),
        P(("dp", "expert"), None),
        P(("dp", "expert")),
        P("expert", None, "dp", None),
        P("expert", None, "dp"),
        P("expert", None, "dp"),
    )
    return jax.shard_map(
        body,
        mesh=mesh,
        in_specs=placed,
        out_specs=(P("expert", None, "dp"), P("expert", None, "dp")),
        check_vma=False,
    )
```

time: 195 us -> 133 us (0.68)
  blocking collectives: 83.3 us -> 0 us
  Pallas kernels: 100 us -> 128 us
  other arithmetic: 4.78 us -> 0 us
    all_gather x3 -> x0, blocking collectives: 83.3 us -> none  [the longest x1 38.3 us: body(): lax.all_gather(packed, 'expert', axis=0, tiled=False)]
    pallas_call x2 -> x1, Pallas kernels: 100 us -> 128 us  [body(): pl.pallas_call(functools.partial(step_kernel, zs, total), out_shape=(jax....]
where the time goes in v2:
time: 133 us; the launch traced here: 132 us
  Pallas kernels  128 us (96%)
  local copies, waits for them, and re-layouts  3.88 us (3%)
    pallas_call x1, Pallas kernels, body(): pl.pallas_call(functools.partial(step_kernel, zs, total), out_shape=(jax....  128 us

profile of v2, /device:TPU:1, one launch (start us, length us, event | category | flops | bytes accessed | tf_op | source)
XLA Modules:
  0.0 132.4 jit_solution(9678147124406881929)
XLA Ops:
  0.6 1.3 copy.9.mate_ref
  1.9 127.9 %lorra_step.1 = (f32[8,96]{1,0:T(8,128)}, f32[8,320]{1,0:T(8,128)}) custom-call(bf16[4,5120]{1,0:T(4,128)(2,1)} %tok_ref.1, s32[4,6]{1,0:T(4,128)} %ids_ref.1, f32[4,6]{1,0:T(4,128)} %route_ref.1, s32[4,1]{1,0:T(4,128)} %copy.9.mate_ref, bf16[2,96,5120]{2,1,0:T(8,128)(2,1)} %bitcast.6, bf16[8,96]{1,0:T(8,128)(2,1)} %bitcast.10, bf16[8,320]{1,0:T(8,128)(2,1)} %bitcast.8), custom_call_target="tpu_custom_call" | custom-call | tf_op jit(solution)/shard_map/lorra_step/pallas_call | solution.py:476
  129.8 1.3 copy.12
  131.1 1.3 copy.13

commit v3 on v2

v3 whole, which is shorter than its diff:
```python
import functools
import math

import jax
import jax.numpy as jnp
from jax import lax
from jax.experimental import pallas as pl
from jax.experimental.pallas import tpu as pltpu
from jax.sharding import PartitionSpec as P

SCALE = 2.0
CONTROL = 0.5
SIDE = 4
SHARE = 1536
HIGH = lax.Precision.HIGHEST
MESH = pl.DeviceIdType.MESH
F32 = jnp.float32
BF16 = jnp.bfloat16


def dot_t(a, b, **kw):
    return lax.dot_general(a, b, (((1,), (1,)), ((), ())), preferred_element_type=F32, **kw)


def split(v):
    hi = v.astype(BF16)
    lo = (v - hi.astype(F32)).astype(BF16)
    return hi, lo


def step_kernel(
    zs, total, share, tok_ref, ids_ref, route_ref, mate_ref, w_ref, adn_ref, aup_ref, out_ref,
    zg, zq, xf, xt, xg, tab, pk, pks, apair, apad, aall, bd, gsend, grecv,
    xall, wbuf, accg, accu, hid, lowp, lowr, lown, lowz, val, ct, msgs, met, cot, chat, half, taken,
    ssem, rsem, lsem, wssem, wrsem, asend, arecv, rsend, rrecv, lsend, lrecv, qsend, qrecv,
    pssend, psrecv, prsend, prrecv,
    azsend, azrecv, gssem, grsem, psend, precv, zsend, zrecv, msend, mrecv, csend, crecv,
):
    count, d_model = tok_ref.shape
    part = d_model - share
    d_half = part // 2
    quarter = d_half // 2
    units = w_ref.shape[1]
    width = aup_ref.shape[1]
    aw = apair.shape[1]
    tokens = zs * count
    experts = 2 * zs
    wide = zs * 16
    factor = 2.0 / math.sqrt(total)
    qz = zq.shape[0]
    nq = zs // qz
    qrows = qz * count
    slice_w = share // qz
    dp = lax.axis_index("dp")
    ex = lax.axis_index("expert")
    y, x = dp // SIDE, lax.rem(dp, SIDE)
    z, c = ex // 2, lax.rem(ex, 2)
    a, b = z // qz, lax.rem(z, qz)
    other = 2 * z + (1 - c)
    groups = SIDE * SIDE

    barrier = pltpu.get_barrier_semaphore()

    def greet_dp(k, carry):
        pl.semaphore_signal(barrier, inc=1, device_id={"dp": lax.rem(dp + k, groups)}, device_id_type=MESH)
        return carry

    def greet_z(k, carry):
        pl.semaphore_signal(
            barrier, inc=1, device_id={"expert": 2 * lax.rem(z + k, zs) + c}, device_id_type=MESH
        )
        return carry

    lax.fori_loop(1, zs, greet_z, 0)
    pl.semaphore_signal(barrier, inc=1, device_id={"expert": other}, device_id_type=MESH)
    lax.fori_loop(1, groups, greet_dp, 0)

    weights = []
    for g in range(2):
        mine = pltpu.make_async_copy(w_ref.at[g], wbuf.at[g, pl.ds(0, units)], lsem.at[g])
        mine.start()
        weights.append(mine)
    col = lax.broadcasted_iota(jnp.int32, (count, 128), 1)
    row4 = lax.broadcasted_iota(jnp.int32, (count, 128), 0)
    named = lax.rem(col, experts)
    wtab = jnp.zeros((count, 128), F32)
    for k in range(ids_ref.shape[1]):
        place_of = jnp.bitwise_xor(ids_ref[:, k : k + 1], c)
        wtab = wtab + jnp.where(named == place_of, route_ref[:, k : k + 1], 0.0)
    top = wtab.astype(BF16).astype(F32)
    mid = (wtab - top).astype(BF16).astype(F32)
    rest = wtab - top - mid
    pick = jnp.zeros((count, 128), F32)
    for k in range(count):
        pick = jnp.where((row4 == k) & (col - 3 * experts == mate_ref[k]), 1.0, pick)
    packed = jnp.where(
        col < experts, top, jnp.where(col < 2 * experts, mid, jnp.where(col < 3 * experts, rest, pick))
    )
    zq[b] = tok_ref[...]
    zg[z, :, 0:part] = tok_ref[:, 0:part]
    zg[z, :, part : part + 128] = packed.astype(BF16)
    pk[...] = jnp.zeros_like(pk)
    pk[:, 0:width] = aup_ref[...]
    pk[:, aw : aw + units] = adn_ref[...]
    accg[...] = jnp.zeros_like(accg)
    accu[...] = jnp.zeros_like(accu)

    pl.semaphore_wait(barrier, groups + zs - 1)

    def zdev(step):
        return {"expert": 2 * lax.rem(z + step + zs, zs) + c}

    def quad_copy(k):
        return pltpu.make_async_remote_copy(
            src_ref=zq.at[b], dst_ref=zq.at[b], send_sem=qsend.at[k], recv_sem=qrecv.at[k],
            device_id={"expert": 2 * (a * qz + lax.rem(b + k, qz)) + c}, device_id_type=MESH,
        )

    def quad_arrived(k):
        slot = lax.rem(b - k + qz, qz)
        pltpu.make_async_remote_copy(
            src_ref=zq.at[slot], dst_ref=zq.at[slot], send_sem=qsend.at[k], recv_sem=qrecv.at[k],
            device_id={"expert": 2 * (a * qz + slot) + c}, device_id_type=MESH,
        ).wait_recv()

    def line(step, s):
        block = lax.rem(z - step * s + zs, zs)
        return pltpu.make_async_remote_copy(
            src_ref=zg.at[block], dst_ref=zg.at[block],
            send_sem=(rsend if step > 0 else lsend).at[s], recv_sem=(rrecv if step > 0 else lrecv).at[s],
            device_id=zdev(step), device_id_type=MESH,
        )

    def landed(step, s):
        block = lax.rem(z - step * (s + 1) + zs, zs)
        pltpu.make_async_remote_copy(
            src_ref=zg.at[block], dst_ref=zg.at[block],
            send_sem=(rsend if step > 0 else lsend).at[s], recv_sem=(rrecv if step > 0 else lrecv).at[s],
            device_id=zdev(step), device_id_type=MESH,
        ).wait_recv()

    reach = {1: zs // 2, -1: zs - 1 - zs // 2}

    def hop(s):
        for step in (1, -1):
            if 1 <= s <= reach[step]:
                landed(step, s - 1)
            if s < reach[step]:
                line(step, s).start()

    hop(0)
    for k in range(1, qz):
        quad_copy(k).start()
    swap_a = pltpu.make_async_remote_copy(
        src_ref=pk, dst_ref=pks, send_sem=asend, recv_sem=arecv,
        device_id={"expert": other}, device_id_type=MESH,
    )
    swap_a.start()
    for g in range(2):
        theirs = pltpu.make_async_remote_copy(
            src_ref=w_ref.at[g], dst_ref=wbuf.at[g, pl.ds(units, units)],
            send_sem=wssem.at[g], recv_sem=wrsem.at[g],
            device_id={"expert": other}, device_id_type=MESH,
        )
        theirs.start()
        weights.append(theirs)

    def far(h, first, step):
        along_x = (h == 0) == first
        yy = y if along_x else lax.rem(y + step + SIDE, SIDE)
        xx = lax.rem(x + step + SIDE, SIDE) if along_x else x
        return {"dp": yy * SIDE + xx}

    def place(h, da, db):
        dx, dy = (da, db) if h == 0 else (db, da)
        return lax.rem(y + dy + SIDE, SIDE), lax.rem(x + dx + SIDE, SIDE)

    def cols(h, piece):
        lo = h * d_half
        if piece is None:
            return pl.ds(lo, d_half)
        return pl.ds(lo + piece * quarter, quarter)

    started = []
    span = (pl.ds(0, qrows), pl.ds(qrows, tokens - qrows))
    offsets = (0, -1, 1, 2)

    def number(stage, h, phase, j, kind):
        return stage * 40 + h * 20 + (kind if phase == 0 else 4 + 4 * j + kind)

    def send(stage, h, da, db, piece, first, step, at):
        by, bx = place(h, da, db)
        block = xall.at[by, bx, span[stage], cols(h, piece)]
        source = xg.at[span[stage], cols(h, piece)] if da == 0 and db == 0 else block
        copy = pltpu.make_async_remote_copy(
            src_ref=source, dst_ref=block, send_sem=ssem.at[at], recv_sem=rsem.at[at],
            device_id=far(h, first, step), device_id_type=MESH,
        )
        copy.start()
        started.append(copy)

    def arrived(stage, h, da, db, piece, at):
        by, bx = place(h, da, db)
        block = xall.at[by, bx, span[stage], cols(h, piece)]
        pltpu.make_async_remote_copy(
            src_ref=block, dst_ref=block, send_sem=ssem.at[at], recv_sem=rsem.at[at],
            device_id=far(h, True, 1), device_id_type=MESH,
        ).wait_recv()

    def xy_own(stage):
        for phase in (0, 1):
            for h in range(2):
                for kind, step in ((0, 1), (1, -1)):
                    send(stage, h, 0, 0, None, phase == 0, step, number(stage, h, phase, 0, kind))
        copy = pltpu.make_async_copy(
            xg.at[span[stage], pl.ds(0, part)], xall.at[y, x, span[stage], pl.ds(0, part)], lsem.at[2 + stage]
        )
        copy.start()
        return copy

    def xy_near(stage):
        for h in range(2):
            arrived(stage, h, -1, 0, None, number(stage, h, 0, 0, 0))
            send(stage, h, -1, 0, 0, True, 1, number(stage, h, 0, 0, 2))
            arrived(stage, h, 1, 0, None, number(stage, h, 0, 0, 1))
            send(stage, h, 1, 0, 1, True, -1, number(stage, h, 0, 0, 3))
            for j in (1, 2):
                send(stage, h, offsets[j], 0, None, False, 1, number(stage, h, 1, j, 0))
                send(stage, h, offsets[j], 0, None, False, -1, number(stage, h, 1, j, 1))

    def xy_far(stage):
        for h in range(2):
            arrived(stage, h, 2, 0, 0, number(stage, h, 0, 0, 2))
            arrived(stage, h, 2, 0, 1, number(stage, h, 0, 0, 3))
            send(stage, h, 2, 0, None, False, 1, number(stage, h, 1, 3, 0))
            send(stage, h, 2, 0, None, False, -1, number(stage, h, 1, 3, 1))

    def xy_pass(stage, j):
        for h in range(2):
            arrived(stage, h, offsets[j], -1, None, number(stage, h, 1, j, 0))
            send(stage, h, offsets[j], -1, 0, False, 1, number(stage, h, 1, j, 2))
            arrived(stage, h, offsets[j], 1, None, number(stage, h, 1, j, 1))
            send(stage, h, offsets[j], 1, 1, False, -1, number(stage, h, 1, j, 3))

    def xy_last(stage, h):
        for j in range(4):
            arrived(stage, h, offsets[j], 2, 0, number(stage, h, 1, j, 2))
            arrived(stage, h, offsets[j], 2, 1, number(stage, h, 1, j, 3))

    strip_cols = pl.ds(pl.multiple_of(part + b * slice_w, 128), slice_w)

    def spread_copy(k):
        return pltpu.make_async_remote_copy(
            src_ref=xg.at[pl.ds(0, qrows), strip_cols],
            dst_ref=xall.at[y, x, pl.ds(0, qrows), strip_cols],
            send_sem=pssend.at[k], recv_sem=psrecv.at[k],
            device_id={"dp": lax.rem(dp + k, groups)}, device_id_type=MESH,
        )

    def spread_arrived(k):
        source = lax.rem(dp - k + groups, groups)
        block = xall.at[source // SIDE, lax.rem(source, SIDE), pl.ds(0, qrows), strip_cols]
        pltpu.make_async_remote_copy(
            src_ref=block, dst_ref=block, send_sem=pssend.at[k], recv_sem=psrecv.at[k],
            device_id={"dp": source}, device_id_type=MESH,
        ).wait_recv()

    def piece_at(source, holder, sub):
        theirs = lax.rem(source // qz - holder // qz + nq, nq)
        return xall.at[
            pl.ds(2 * sub, 2), :, pl.ds(pl.multiple_of(qrows * theirs, qrows), qrows),
            pl.ds(pl.multiple_of(part + lax.rem(source, qz) * slice_w, 128), slice_w),
        ]

    def ring_slot(step, s, sub):
        return (0 if step > 0 else 2 * (zs // 2)) + 2 * s + sub

    def ring_copy(step, s, sub):
        source = lax.rem(z - step * s + zs, zs)
        peer = lax.rem(z + step + zs, zs)
        at = ring_slot(step, s, sub)
        return pltpu.make_async_remote_copy(
            src_ref=piece_at(source, z, sub), dst_ref=piece_at(source, peer, sub),
            send_sem=prsend.at[at], recv_sem=prrecv.at[at], device_id=zdev(step), device_id_type=MESH,
        )

    def ring_landed(step, s, sub):
        source = lax.rem(z - step * (s + 1) + zs, zs)
        at = ring_slot(step, s, sub)
        block = piece_at(source, z, sub)
        pltpu.make_async_remote_copy(
            src_ref=block, dst_ref=block,
            send_sem=prsend.at[at], recv_sem=prrecv.at[at], device_id=zdev(step), device_id_type=MESH,
        ).wait_recv()

    def ring(s):
        for sub in range(2):
            for step in (1, -1):
                if 1 <= s <= reach[step]:
                    ring_landed(step, s - 1, sub)
                if s < reach[step]:
                    ring_copy(step, s, sub).start()

    hop(1)
    for k in range(1, qz):
        quad_arrived(k)
    for k in range(qz):
        xf[count * k : count * (k + 1), :] = zq[k].astype(F32)
    xg[0:qrows, :] = xf[0:qrows, :].astype(BF16)

    def start_spread(k, carry):
        spread_copy(k).start()
        return carry

    def wait_spread(k, carry):
        spread_arrived(k)
        return carry

    lax.fori_loop(1, groups, start_spread, 0)
    mine_q = pltpu.make_async_copy(
        xg.at[pl.ds(0, qrows), strip_cols], xall.at[y, x, pl.ds(0, qrows), strip_cols], lsem.at[4]
    )
    mine_q.start()
    own0 = xy_own(0)
    hop(2)

    swap_a.wait()
    lead, follow = pk[...].astype(F32), pks[...].astype(F32)
    stacked = jnp.concatenate([lead, follow], axis=0)
    apair[...] = stacked[:, 0:aw].astype(BF16)
    aall[z] = stacked[:, 0:aw].astype(BF16)
    spread = jnp.concatenate([stacked[:, 0:width], jnp.zeros((16, width), F32)], axis=1)
    odd = jnp.concatenate([jnp.zeros((16, width), F32), stacked[:, 0:width]], axis=1)
    apad[...] = jnp.where(lax.rem(dp, 2) == 0, spread, odd).astype(BF16)
    blank = jnp.zeros((8, units), F32)
    bd[...] = jnp.concatenate(
        [
            jnp.concatenate([lead[:, aw : aw + units], blank], axis=1),
            jnp.concatenate([blank, follow[:, aw : aw + units]], axis=1),
        ],
        axis=0,
    ).astype(BF16)

    def a_copy(k):
        return pltpu.make_async_remote_copy(
            src_ref=apair, dst_ref=aall.at[z], send_sem=azsend.at[k], recv_sem=azrecv.at[k],
            device_id=zdev(k), device_id_type=MESH,
        )

    def a_arrival(k):
        source = lax.rem(z - k + zs, zs)
        return pltpu.make_async_remote_copy(
            src_ref=apair, dst_ref=aall.at[source], send_sem=azsend.at[k], recv_sem=azrecv.at[k],
            device_id={"expert": 2 * source + c}, device_id_type=MESH,
        )

    def start_a(k, carry):
        a_copy(k).start()
        return carry

    def wait_a(k, carry):
        a_arrival(k).wait_recv()
        a_copy(k).wait_send()
        return carry

    def g_copy(k):
        return pltpu.make_async_remote_copy(
            src_ref=gsend, dst_ref=grecv.at[k], send_sem=gssem.at[k], recv_sem=grsem.at[k],
            device_id={"dp": lax.rem(dp + k, groups)}, device_id_type=MESH,
        )

    def start_g(k, carry):
        g_copy(k).start()
        return carry

    def wait_g(k, carry):
        g_copy(k).wait()
        return carry + grecv[k].astype(F32)

    steps = zs // 2
    early = {
        3: lambda: xy_near(0),
        5: lambda: xy_far(0),
        6: lambda: xy_pass(0, 0),
        7: lambda: xy_pass(0, 1),
    }
    for s in range(3, steps + 1):
        hop(s)
        if s == 4:
            mine_q.wait()
            lax.fori_loop(1, groups, wait_spread, 0)
            ring(0)
        if s == 6:
            ring(1)
        if s in early:
            early[s]()
    late = [s for s in sorted(early) if s > steps]

    order = [lax.rem(a + rho, nq) * qz + k for rho in range(nq) for k in range(qz)]
    for at, source in enumerate(order):
        xt[count * at : count * (at + 1), :] = zg[source, :, part : part + 128].astype(F32)
        if at >= qz:
            xf[count * at : count * (at + 1), 0:part] = zg[source, :, 0:part].astype(F32)
    xg[qrows:tokens, 0:part] = xf[qrows:tokens, 0:part].astype(BF16)
    tab[...] = xt[...].astype(BF16)
    own1 = xy_own(1)
    if steps < 4:
        mine_q.wait()
        lax.fori_loop(1, groups, wait_spread, 0)
        ring(0)
    if steps < 6:
        ring(1)
    for s in late:
        early[s]()
    lax.fori_loop(1, zs, start_a, 0)
    ring(2)
    xy_pass(0, 2)
    xy_near(1)
    xy_pass(0, 3)
    ring(3)
    xy_far(1)
    own0.wait()
    own1.wait()
    for copy in weights:
        copy.wait()
    for h in range(2):
        xy_last(0, h)

    def panel(block, at):
        return [dot_t(block, wbuf[g, :, at]) for g in range(2)]

    chunk = 512 if d_half % 512 == 0 else 256 if d_half % 256 == 0 else 128
    while chunk * 2 <= 1024 and d_half % (chunk * 2) == 0:
        chunk *= 2
    rows = SIDE * tokens

    def multiply(h, db):
        by, bx = place(h, 0, db)

        def step(i, carry):
            at = pl.ds(pl.multiple_of(h * d_half + i * chunk, 128), chunk)
            if h == 0:
                block = xall[by, :, :, at]
            else:
                block = xall[:, bx, :, at]
            for acc, value in zip((accg, accu), panel(block.reshape(rows, chunk), at)):
                value = value.reshape(SIDE, tokens, 2 * units)
                if h == 0:
                    acc[by] = acc[by] + value
                else:
                    acc[:, bx] = acc[:, bx] + value
            return carry

        lax.fori_loop(0, d_half // chunk, step, 0)

    def multiply_q(lo, hi):
        size = (hi - lo) * qrows

        def step(i, carry):
            at = pl.ds(pl.multiple_of(part + i * slice_w, 128), slice_w)
            block = xall[:, :, lo * qrows : hi * qrows, at].reshape(groups * size, slice_w)
            for acc, value in zip((accg, accu), panel(block, at)):
                where = (slice(None), slice(None), slice(lo * qrows, hi * qrows))
                acc[where] = acc[where] + value.reshape(SIDE, SIDE, size, 2 * units)
            return carry

        lax.fori_loop(0, qz, step, 0)

    xy_pass(1, 0)
    ring(4)
    lax.fori_loop(1, zs, wait_a, 0)
    gsend[...] = dot_t(apair[...], aall[...].reshape(wide, aw)).astype(BF16)
    lax.fori_loop(1, groups, start_g, 0)
    multiply(0, 0)
    xy_pass(1, 1)
    ring(5)
    multiply(1, 0)
    xy_pass(1, 2)
    ring(6)
    xy_pass(1, 3)
    ring(7)
    multiply(0, -1)
    multiply(0, 1)
    multiply(1, -1)
    multiply(1, 1)
    ring(8)
    multiply_q(0, nq)
    gmat = lax.fori_loop(1, groups, wait_g, gsend[...].astype(F32))
    for h in range(2):
        xy_last(1, h)
        multiply(h, 2)

    both = accg.shape[3]
    gate = accg[...].reshape(groups * tokens, both)
    hid[...] = (gate * (1.0 / (1.0 + jnp.exp(-gate))) * accu[...].reshape(groups * tokens, both)).astype(BF16)
    strip = pl.ds(pl.multiple_of(2 * width * (dp // 2), 128), 2 * width)
    low = dot_t(bd[...], hid[...])
    tall = dot_t(apad[...], xall[:, :, :, strip].reshape(groups * tokens, 2 * width))
    for k in range(groups):
        lowp[k, :, 0:tokens] = low[:, k * tokens : (k + 1) * tokens]
        lowp[k, :, 64 : 64 + tokens] = tall[:, k * tokens : (k + 1) * tokens]

    def low_copy(k):
        peer = lax.rem(dp + k, groups)
        return pltpu.make_async_remote_copy(
            src_ref=lowp.at[peer], dst_ref=lowr.at[k], send_sem=psend.at[k], recv_sem=precv.at[k],
            device_id={"dp": peer}, device_id_type=MESH,
        )

    def start_low(k, carry):
        low_copy(k).start()
        return carry

    def wait_low(k, carry):
        low_copy(k).wait()
        return carry + lowr[k]

    lax.fori_loop(1, groups, start_low, 0)
    row = lax.broadcasted_iota(jnp.int32, (wide, 128), 0)
    lane = lax.broadcasted_iota(jnp.int32, (wide, 128), 1)
    chooser = jnp.where((row // 8 == lax.rem(lane, experts)) & (lane < 3 * experts), 1.0, 0.0).astype(BF16)
    w8 = dot_t(chooser, tab[...])
    trow = lax.broadcasted_iota(jnp.int32, (tokens, 128), 0)
    tlane = lax.broadcasted_iota(jnp.int32, (tokens, 128), 1)
    finder = jnp.where(tlane - 3 * experts == lax.rem(trow, count), 1.0, 0.0).astype(BF16)
    t0 = lax.broadcasted_iota(jnp.int32, (tokens, tokens), 0)
    t1 = lax.broadcasted_iota(jnp.int32, (tokens, tokens), 1)
    mate = jnp.where(t0 // count == t1 // count, dot_t(finder, tab[...]), 0.0)
    q = jnp.where(t0 == t1, 1.0, 0.0) - mate
    summed = lax.fori_loop(1, groups, wait_low, lowp[dp])
    lown[:, 0:tokens] = summed[0:8, 0:tokens]
    lown[:, 64 : 64 + tokens] = summed[8:16, 0:tokens]

    def z_copy(k):
        return pltpu.make_async_remote_copy(
            src_ref=lown, dst_ref=lowz.at[z], send_sem=zsend.at[k], recv_sem=zrecv.at[k],
            device_id=zdev(k), device_id_type=MESH,
        )

    def z_arrival(k):
        source = lax.rem(z - k + zs, zs)
        return pltpu.make_async_remote_copy(
            src_ref=lown, dst_ref=lowz.at[source], send_sem=zsend.at[k], recv_sem=zrecv.at[k],
            device_id={"expert": 2 * source + c}, device_id_type=MESH,
        )

    def start_z(k, carry):
        z_copy(k).start()
        return carry

    def wait_z(k, carry):
        z_arrival(k).wait_recv()
        return carry

    def done_z(k, carry):
        z_copy(k).wait_send()
        return carry

    lax.fori_loop(1, zs, start_z, 0)
    lowz[z] = lown[...]
    zt = jnp.dot(summed[:, 64 : 64 + tokens], q, precision=HIGH, preferred_element_type=F32)
    lax.fori_loop(1, zs, wait_z, 0)

    for rho in range(nq):
        there = pl.ds(qz * lax.rem(a + rho, nq), qz)
        found = lowz[there]
        turn = qrows * rho
        for o in range(2):
            lanes = found[:, :, 64 * o : 64 * o + tokens]
            if turn:
                lanes = jnp.concatenate([lanes[:, :, tokens - turn :], lanes[:, :, : tokens - turn]], axis=2)
            val[there, 8 * o : 8 * o + 8, 0:tokens] = lanes
    values = val[...].reshape(wide, 128)[:, 0:tokens] * w8
    ct[:, 0:tokens] = values
    ct[:, 64 : 64 + tokens] = w8
    here = pl.ds(pl.multiple_of(16 * z, 16), 16)
    mine = ct[here, 0:tokens]
    weight = ct[here, 64 : 64 + tokens]
    inner = jnp.dot(gmat, values, precision=HIGH, preferred_element_type=F32)
    first = weight * (factor * (SCALE * inner - CONTROL * zt))
    second = jnp.dot(mine, q, precision=HIGH, preferred_element_type=F32)
    msgs[:, 0 : 2 * tokens] = jnp.concatenate([first, second], axis=1).astype(BF16)
    msgs[:, 2 * tokens : 2 * tokens + wide] = dot_t(mine, values, precision=HIGH).astype(BF16)

    def m_copy(k):
        return pltpu.make_async_remote_copy(
            src_ref=msgs, dst_ref=met.at[k], send_sem=msend.at[k], recv_sem=mrecv.at[k],
            device_id={"dp": lax.rem(dp + k, groups)}, device_id_type=MESH,
        )

    def start_m(k, carry):
        m_copy(k).start()
        return carry

    def wait_m(k, carry):
        m_copy(k).wait()
        return carry + met[k, :, 2 * tokens : 2 * tokens + wide].astype(F32)

    lax.fori_loop(1, groups, start_m, 0)
    met[0] = msgs[...]
    lax.fori_loop(1, zs, done_z, 0)
    for step in (1, -1):
        for s in range(reach[step]):
            line(step, s).wait_send()
            for sub in range(2):
                ring_copy(step, s, sub).wait_send()
    for k in range(1, qz):
        quad_copy(k).wait_send()

    def done_spread(k, carry):
        spread_copy(k).wait_send()
        return carry

    lax.fori_loop(1, groups, done_spread, 0)
    for copy in started:
        copy.wait_send()
    gram = lax.fori_loop(1, groups, wait_m, msgs[:, 2 * tokens : 2 * tokens + wide].astype(F32))
    for k in range(groups):
        block = met[lax.rem(dp - k + groups, groups), :, 0 : 2 * tokens].astype(F32)
        cot[:, k * tokens : (k + 1) * tokens] = block[:, 0:tokens]
        chat[:, k * tokens : (k + 1) * tokens] = block[:, tokens : 2 * tokens]

    down = SCALE * jnp.dot(cot[...].astype(BF16), hid[...], preferred_element_type=F32)
    along = jnp.dot(
        chat[...].astype(BF16), xall[:, :, :, strip].reshape(groups * tokens, 2 * width),
        preferred_element_type=F32,
    )
    along = jnp.where(lax.rem(dp, 2) == 0, along[:, 0:width], along[:, width : 2 * width])
    slices = aall[...].reshape(wide, aw)
    hi, lo = split(gram)
    through = jnp.dot(hi, slices, preferred_element_type=F32) + jnp.dot(lo, slices, preferred_element_type=F32)
    up = (SCALE * factor) * (SCALE * through[:, 0:width] - CONTROL * along)
    half[:, 0:units] = down[8:16, units : 2 * units]
    half[:, 128 : 128 + width] = up[8:16, :]
    swap = pltpu.make_async_remote_copy(
        src_ref=half, dst_ref=taken, send_sem=csend, recv_sem=crecv,
        device_id={"expert": other}, device_id_type=MESH,
    )
    swap.start()
    swap.wait()
    out_ref[...] = jnp.zeros_like(out_ref)
    out_ref[:, 0:units] = down[0:8, 0:units] + taken[:, 0:units]
    out_ref[:, 128 : 128 + width] = up[0:8, :] + taken[:, 128 : 128 + width]


def part_kernel(both_ref, down_ref, up_ref):
    down_ref[...] = both_ref[:, 0 : down_ref.shape[1]]
    up_ref[...] = both_ref[:, 128 : 128 + up_ref.shape[1]]


def whole(space=pltpu.VMEM):
    return pl.BlockSpec(memory_space=space)


def body(tokens, chosen, router, partner, gate_up, a_down, a_up):
    count, d_model = tokens.shape
    groups = lax.axis_size("dp")
    experts = lax.axis_size("expert")
    zs = experts // 2
    units = gate_up.shape[2]
    width = a_up.shape[2]
    rank = a_up.shape[1]
    gtok = zs * count
    wide = zs * 16
    qz = 4 if zs >= 8 else 2
    share = SHARE if d_model == 5120 else d_model // 2
    aw = -(-width // 128) * 128
    mw = 2 * gtok + max(128, wide)
    total = count * groups * experts
    dma = pltpu.SemaphoreType.DMA
    out = pl.pallas_call(
        functools.partial(step_kernel, zs, total, share),
        out_shape=jax.ShapeDtypeStruct((rank, 128 + aw), F32),
        in_specs=[whole()] * 3 + [whole(pltpu.SMEM), whole(pl.ANY)] + [whole()] * 2,
        out_specs=whole(),
        scratch_shapes=[
            pltpu.VMEM((zs, count, d_model - share + 128), BF16),
            pltpu.VMEM((qz, count, d_model), BF16),
            pltpu.VMEM((gtok, d_model), F32),
            pltpu.VMEM((gtok, 128), F32),
            pltpu.VMEM((gtok, d_model), BF16),
            pltpu.VMEM((gtok, 128), BF16),
            pltpu.VMEM((rank, aw + 128), BF16),
            pltpu.VMEM((rank, aw + 128), BF16),
            pltpu.VMEM((16, aw), BF16),
            pltpu.VMEM((16, 2 * width), BF16),
            pltpu.VMEM((zs, 16, aw), BF16),
            pltpu.VMEM((16, 2 * units), BF16),
            pltpu.VMEM((16, wide), BF16),
            pltpu.VMEM((groups, 16, wide), BF16),
            pltpu.VMEM((SIDE, SIDE, gtok, d_model), BF16),
            pltpu.VMEM((2, 2 * units, d_model), BF16),
            pltpu.VMEM((SIDE, SIDE, gtok, 2 * units), F32),
            pltpu.VMEM((SIDE, SIDE, gtok, 2 * units), F32),
            pltpu.VMEM((groups * gtok, 2 * units), BF16),
            pltpu.VMEM((groups, 16, 128), F32),
            pltpu.VMEM((groups, 16, 128), F32),
            pltpu.VMEM((8, 128), F32),
            pltpu.VMEM((zs, 8, 128), F32),
            pltpu.VMEM((zs, 16, 128), F32),
            pltpu.VMEM((wide, 128), F32),
            pltpu.VMEM((16, mw), BF16),
            pltpu.VMEM((groups, 16, mw), BF16),
            pltpu.VMEM((16, groups * gtok), F32),
            pltpu.VMEM((16, groups * gtok), F32),
            pltpu.VMEM((8, 128 + aw), F32),
            pltpu.VMEM((8, 128 + aw), F32),
            dma((80,)), dma((80,)), dma((5,)), dma((2,)), dma((2,)), dma, dma,
            dma((zs,)), dma((zs,)), dma((zs,)), dma((zs,)), dma((qz,)), dma((qz,)),
            dma((groups,)), dma((groups,)), dma((2 * zs,)), dma((2 * zs,)),
            dma((zs,)), dma((zs,)), dma((groups,)), dma((groups,)), dma((groups,)), dma((groups,)),
            dma((zs,)), dma((zs,)), dma((groups,)), dma((groups,)), dma, dma,
        ],
        compiler_params=pltpu.CompilerParams(
            collective_id=0, has_side_effects=True, vmem_limit_bytes=56 << 20
        ),
        name="lorra_step",
    )(tokens, chosen, router, partner, gate_up[0], a_down[0], a_up[0])
    down, up = pl.pallas_call(
        part_kernel,
        out_shape=(
            jax.ShapeDtypeStruct((rank, units), F32),
            jax.ShapeDtypeStruct((rank, width), F32),
        ),
        in_specs=[whole()],
        out_specs=(whole(), whole()),
        name="part",
    )(out)
    return (down[None], up[None])


def solution(mesh):
    placed = (
        P(("dp", "expert"), None),
        P(("dp", "expert"), None),
        P(("dp", "expert"), None),
        P(("dp", "expert")),
        P("expert", None, "dp", None),
        P("expert", None, "dp"),
        P("expert", None, "dp"),
    )
    return jax.shard_map(
        body,
        mesh=mesh,
        in_specs=placed,
        out_specs=(P("expert", None, "dp"), P("expert", None, "dp")),
        check_vma=False,
    )
```

time: 133 us -> 124 us (0.932)
  Pallas kernels: 128 us -> 123 us
  local copies, waits for them, and re-layouts: 3.88 us -> 0 us
    pallas_call x1 -> x2, Pallas kernels: 128 us -> 123 us  [the longest x1 121 us: body(): pl.pallas_call(functools.partial(step_kernel, zs, total, share), out_shap...]
    unnamed x2 -> x0, local copies, waits for them, and re-layouts: 2.57 us -> none
where the time goes in v3:
time: 124 us; the launch traced here: 123 us
  Pallas kernels  123 us (99%)
    pallas_call x1, Pallas kernels, body(): pl.pallas_call(functools.partial(step_kernel, zs, total, share), out_shap...  121 us

profile of v3, /device:TPU:1, one launch (start us, length us, event | category | flops | bytes accessed | tf_op | source)
XLA Modules:
  0.0 123.4 jit_solution(3202020148262095767)
XLA Ops:
  0.6 121.4 %lorra_step.1.both_ref = f32[8,512]{1,0:T(8,128)} custom-call(bf16[4,5120]{1,0:T(4,128)(2,1)} %tok_ref.1, s32[4,6]{1,0:T(4,128)} %ids_ref.1, f32[4,6]{1,0:T(4,128)} %route_ref.1, s32[4]{0:T(128)} %mate_ref.1, bf16[2,96,5120]{2,1,0:T(8,128)(2,1)} %bitcast.5, bf16[8,96]{1,0:T(8,128)(2,1)} %bitcast.7, bf16[8,320]{1,0:T(8,128)(2,1)} %bitcast.6), custom_call_target="tpu_custom_call" | custom-call | tf_op jit(solution)/shard_map/lorra_step/pallas_call | solution.py:671
  122.1 1.3 %part.1 = (f32[8,96]{1,0:T(8,128)}, f32[8,320]{1,0:T(8,128)}) custom-call(f32[8,512]{1,0:T(8,128)} %lorra_step.1.both_ref), custom_call_target="tpu_custom_call" | custom-call | tf_op jit(solution)/shard_map/part/pallas_call | solution.py:719

commit v4 on v3

--- a/solution.py
+++ b/solution.py
@@ -56,6 +56,8 @@
     y, x = dp // SIDE, lax.rem(dp, SIDE)
     z, c = ex // 2, lax.rem(ex, 2)
     a, b = z // qz, lax.rem(z, qz)
+    up_side = (2 * b) // qz
+    quads = (a, lax.rem(a + 2 * up_side + 3, nq), lax.rem(a + 5 - 2 * up_side, nq), lax.rem(a + 2, nq))
     other = 2 * z + (1 - c)
     groups = SIDE * SIDE
 
@@ -165,6 +167,29 @@
         theirs.start()
         weights.append(theirs)
 
+    def a_line(step, s):
+        block = lax.rem(z - step * s + zs, zs)
+        return pltpu.make_async_remote_copy(
+            src_ref=aall.at[block], dst_ref=aall.at[block],
+            send_sem=azsend.at[(0 if step > 0 else zs // 2) + s], recv_sem=azrecv.at[(0 if step > 0 else zs // 2) + s],
+            device_id=zdev(step), device_id_type=MESH,
+        )
+
+    def a_landed(step, s):
+        block = lax.rem(z - step * (s + 1) + zs, zs)
+        pltpu.make_async_remote_copy(
+            src_ref=aall.at[block], dst_ref=aall.at[block],
+            send_sem=azsend.at[(0 if step > 0 else zs // 2) + s], recv_sem=azrecv.at[(0 if step > 0 else zs // 2) + s],
+            device_id=zdev(step), device_id_type=MESH,
+        ).wait_recv()
+
+    def a_hop(s):
+        for step in (1, -1):
+            if 1 <= s <= reach[step]:
+                a_landed(step, s - 1)
+            if s < reach[step]:
+                a_line(step, s).start()
+
     def far(h, first, step):
         along_x = (h == 0) == first
         yy = y if along_x else lax.rem(y + step + SIDE, SIDE)
@@ -182,7 +207,7 @@
         return pl.ds(lo + piece * quarter, quarter)
 
     started = []
-    span = (pl.ds(0, qrows), pl.ds(qrows, tokens - qrows))
+    span = (pl.ds(0, qrows), pl.ds(qrows, qrows), pl.ds(2 * qrows, 2 * qrows))
     offsets = (0, -1, 1, 2)
 
     def number(stage, h, phase, j, kind):
@@ -266,7 +291,10 @@
         ).wait_recv()
 
     def piece_at(source, holder, sub):
-        theirs = lax.rem(source // qz - holder // qz + nq, nq)
+        gap = lax.rem(source // qz - holder // qz + nq, nq)
+        side = (2 * lax.rem(holder, qz)) // qz
+        odd_gap = lax.rem(gap, 2)
+        theirs = (1 - odd_gap) * (gap // 2) * 3 + odd_gap * (2 - side + (gap // 2) * (2 * side - 1))
         return xall.at[
             pl.ds(2 * sub, 2), :, pl.ds(pl.multiple_of(qrows * theirs, qrows), qrows),
             pl.ds(pl.multiple_of(part + lax.rem(source, qz) * slice_w, 128), slice_w),
@@ -318,7 +346,7 @@
 
     lax.fori_loop(1, groups, start_spread, 0)
     mine_q = pltpu.make_async_copy(
-        xg.at[pl.ds(0, qrows), strip_cols], xall.at[y, x, pl.ds(0, qrows), strip_cols], lsem.at[4]
+        xg.at[pl.ds(0, qrows), strip_cols], xall.at[y, x, pl.ds(0, qrows), strip_cols], lsem.at[5]
     )
     mine_q.start()
     own0 = xy_own(0)
@@ -341,28 +369,6 @@
         axis=0,
     ).astype(BF16)
 
-    def a_copy(k):
-        return pltpu.make_async_remote_copy(
-            src_ref=apair, dst_ref=aall.at[z], send_sem=azsend.at[k], recv_sem=azrecv.at[k],
-            device_id=zdev(k), device_id_type=MESH,
-        )
-
-    def a_arrival(k):
-        source = lax.rem(z - k + zs, zs)
-        return pltpu.make_async_remote_copy(
-            src_ref=apair, dst_ref=aall.at[source], send_sem=azsend.at[k], recv_sem=azrecv.at[k],
-            device_id={"expert": 2 * source + c}, device_id_type=MESH,
-        )
-
-    def start_a(k, carry):
-        a_copy(k).start()
-        return carry
-
-    def wait_a(k, carry):
-        a_arrival(k).wait_recv()
-        a_copy(k).wait_send()
-        return carry
-
     def g_copy(k):
         return pltpu.make_async_remote_copy(
             src_ref=gsend, dst_ref=grecv.at[k], send_sem=gssem.at[k], recv_sem=grsem.at[k],
@@ -377,61 +383,72 @@
         g_copy(k).wait()
         return carry + grecv[k].astype(F32)
 
-    steps = zs // 2
-    early = {
-        3: lambda: xy_near(0),
-        5: lambda: xy_far(0),
-        6: lambda: xy_pass(0, 0),
-        7: lambda: xy_pass(0, 1),
-    }
-    for s in range(3, steps + 1):
-        hop(s)
-        if s == 4:
-            mine_q.wait()
-            lax.fori_loop(1, groups, wait_spread, 0)
-            ring(0)
-        if s == 6:
-            ring(1)
-        if s in early:
-            early[s]()
-    late = [s for s in sorted(early) if s > steps]
-
-    order = [lax.rem(a + rho, nq) * qz + k for rho in range(nq) for k in range(qz)]
-    for at, source in enumerate(order):
-        xt[count * at : count * (at + 1), :] = zg[source, :, part : part + 128].astype(F32)
-        if at >= qz:
-            xf[count * at : count * (at + 1), 0:part] = zg[source, :, 0:part].astype(F32)
-    xg[qrows:tokens, 0:part] = xf[qrows:tokens, 0:part].astype(BF16)
-    tab[...] = xt[...].astype(BF16)
+    def bring(r):
+        for k in range(qz):
+            at = (r * qz + k) * count
+            xf[at : at + count, 0:part] = zg[quads[r] * qz + k, :, 0:part].astype(F32)
+        rows_r = slice(r * qrows, (r + 1) * qrows)
+        xg[rows_r, 0:part] = xf[rows_r, 0:part].astype(BF16)
+
+    a_hop(0)
+    xy_near(0)
+    hop(3)
+    mine_q.wait()
+    lax.fori_loop(1, groups, wait_spread, 0)
+    ring(0)
+    a_hop(1)
+    xy_far(0)
+    hop(4)
+    xy_pass(0, 0)
+    a_hop(2)
+    hop(5)
+    bring(1)
     own1 = xy_own(1)
-    if steps < 4:
-        mine_q.wait()
-        lax.fori_loop(1, groups, wait_spread, 0)
-        ring(0)
-    if steps < 6:
-        ring(1)
-    for s in late:
-        early[s]()
-    lax.fori_loop(1, zs, start_a, 0)
+    ring(1)
+    xy_pass(0, 1)
+    a_hop(3)
+    hop(6)
+    xy_near(1)
     ring(2)
     xy_pass(0, 2)
-    xy_near(1)
+    a_hop(4)
+    hop(7)
+    xy_far(1)
+    ring(3)
     xy_pass(0, 3)
-    ring(3)
-    xy_far(1)
+    a_hop(5)
+    hop(8)
+    bring(2)
+    bring(3)
+    own2 = xy_own(2)
+    for r in range(nq):
+        for k in range(qz):
+            at = (r * qz + k) * count
+            xt[at : at + count, :] = zg[quads[r] * qz + k, :, part : part + 128].astype(F32)
+    tab[...] = xt[...].astype(BF16)
+    xy_pass(1, 0)
+    a_hop(6)
+    ring(4)
+    xy_near(2)
+    xy_pass(1, 1)
+    a_hop(7)
+    for h in range(2):
+        xy_last(0, h)
+    xy_far(2)
+    a_hop(8)
+    ring(5)
     own0.wait()
     own1.wait()
+    own2.wait()
     for copy in weights:
         copy.wait()
-    for h in range(2):
-        xy_last(0, h)
+    xy_pass(1, 2)
+    xy_pass(1, 3)
 
     def panel(block, at):
         return [dot_t(block, wbuf[g, :, at]) for g in range(2)]
 
-    chunk = 512 if d_half % 512 == 0 else 256 if d_half % 256 == 0 else 128
-    while chunk * 2 <= 1024 and d_half % (chunk * 2) == 0:
-        chunk *= 2
+    chunk = d_half
     rows = SIDE * tokens
 
     def multiply(h, db):
@@ -453,41 +470,37 @@
 
         lax.fori_loop(0, d_half // chunk, step, 0)
 
-    def multiply_q(lo, hi):
-        size = (hi - lo) * qrows
+    def multiply_q():
+        at = pl.ds(part, share)
 
         def step(i, carry):
-            at = pl.ds(pl.multiple_of(part + i * slice_w, 128), slice_w)
-            block = xall[:, :, lo * qrows : hi * qrows, at].reshape(groups * size, slice_w)
+            block = xall[i, :, :, at].reshape(rows, share)
             for acc, value in zip((accg, accu), panel(block, at)):
-                where = (slice(None), slice(None), slice(lo * qrows, hi * qrows))
-                acc[where] = acc[where] + value.reshape(SIDE, SIDE, size, 2 * units)
+                acc[i] = acc[i] + value.reshape(SIDE, tokens, 2 * units)
             return carry
 
-        lax.fori_loop(0, qz, step, 0)
-
-    xy_pass(1, 0)
-    ring(4)
-    lax.fori_loop(1, zs, wait_a, 0)
+        lax.fori_loop(0, SIDE, step, 0)
+
+    xy_pass(2, 0)
+    ring(6)
     gsend[...] = dot_t(apair[...], aall[...].reshape(wide, aw)).astype(BF16)
     lax.fori_loop(1, groups, start_g, 0)
     multiply(0, 0)
-    xy_pass(1, 1)
-    ring(5)
+    xy_pass(2, 1)
+    ring(7)
     multiply(1, 0)
-    xy_pass(1, 2)
-    ring(6)
-    xy_pass(1, 3)
-    ring(7)
-    multiply(0, -1)
-    multiply(0, 1)
-    multiply(1, -1)
-    multiply(1, 1)
+    xy_pass(2, 2)
+    for h in range(2):
+        xy_last(1, h)
+    xy_pass(2, 3)
     ring(8)
-    multiply_q(0, nq)
+    for h in range(2):
+        multiply(h, -1)
+        multiply(h, 1)
+    multiply_q()
     gmat = lax.fori_loop(1, groups, wait_g, gsend[...].astype(F32))
     for h in range(2):
-        xy_last(1, h)
+        xy_last(2, h)
         multiply(h, 2)
 
     both = accg.shape[3]
@@ -528,8 +541,18 @@
     mate = jnp.where(t0 // count == t1 // count, dot_t(finder, tab[...]), 0.0)
     q = jnp.where(t0 == t1, 1.0, 0.0) - mate
     summed = lax.fori_loop(1, groups, wait_low, lowp[dp])
-    lown[:, 0:tokens] = summed[0:8, 0:tokens]
-    lown[:, 64 : 64 + tokens] = summed[8:16, 0:tokens]
+
+    def shuffle(v, high, low_side):
+        pieces = [v[:, qrows * i : qrows * (i + 1)] for i in range(nq)]
+        return jnp.where(
+            up_side == 1,
+            jnp.concatenate([pieces[i] for i in high], axis=1),
+            jnp.concatenate([pieces[i] for i in low_side], axis=1),
+        )
+
+    steady = shuffle(summed[:, 0:tokens], (0, 1, 3, 2), (0, 2, 3, 1))
+    lown[:, 0:tokens] = steady[0:8]
+    lown[:, 64 : 64 + tokens] = steady[8:16]
 
     def z_copy(k):
         return pltpu.make_async_remote_copy(
@@ -570,7 +593,7 @@
             if turn:
                 lanes = jnp.concatenate([lanes[:, :, tokens - turn :], lanes[:, :, : tokens - turn]], axis=2)
             val[there, 8 * o : 8 * o + 8, 0:tokens] = lanes
-    values = val[...].reshape(wide, 128)[:, 0:tokens] * w8
+    values = shuffle(val[...].reshape(wide, 128)[:, 0:tokens], (0, 1, 3, 2), (0, 3, 1, 2)) * w8
     ct[:, 0:tokens] = values
     ct[:, 64 : 64 + tokens] = w8
     here = pl.ds(pl.multiple_of(16 * z, 16), 16)
@@ -602,6 +625,7 @@
     for step in (1, -1):
         for s in range(reach[step]):
             line(step, s).wait_send()
+            a_line(step, s).wait_send()
             for sub in range(2):
                 ring_copy(step, s, sub).wait_send()
     for k in range(1, qz):
@@ -662,7 +686,7 @@
     rank = a_up.shape[1]
     gtok = zs * count
     wide = zs * 16
-    qz = 4 if zs >= 8 else 2
+    qz = zs // SIDE
     share = SHARE if d_model == 5120 else d_model // 2
     aw = -(-width // 128) * 128
     mw = 2 * gtok + max(128, wide)
@@ -705,7 +729,7 @@
             pltpu.VMEM((16, groups * gtok), F32),
             pltpu.VMEM((8, 128 + aw), F32),
             pltpu.VMEM((8, 128 + aw), F32),
-            dma((80,)), dma((80,)), dma((5,)), dma((2,)), dma((2,)), dma, dma,
+            dma((120,)), dma((120,)), dma((6,)), dma((2,)), dma((2,)), dma, dma,
             dma((zs,)), dma((zs,)), dma((zs,)), dma((zs,)), dma((qz,)), dma((qz,)),
             dma((groups,)), dma((groups,)), dma((2 * zs,)), dma((2 * zs,)),
             dma((zs,)), dma((zs,)), dma((groups,)), dma((groups,)), dma((groups,)), dma((groups,)),

time: 124 us -> 114 us (0.919)
  Pallas kernels: 123 us -> 113 us
    pallas_call x1, Pallas kernels: 121 us -> 111 us  [body(): pl.pallas_call(functools.partial(step_kernel, zs, total, share), out_shap...]
where the time goes in v4:
time: 114 us; the launch traced here: 113 us
  Pallas kernels  113 us (99%)
    pallas_call x1, Pallas kernels, body(): pl.pallas_call(functools.partial(step_kernel, zs, total, share), out_shap...  111 us

profile of v4, /device:TPU:1, one launch (start us, length us, event | category | flops | bytes accessed | tf_op | source)
XLA Modules:
  0.0 113.3 jit_solution(9761324386412467117)
XLA Ops:
  0.6 111.3 %lorra_step.1.both_ref = f32[8,512]{1,0:T(8,128)} custom-call(bf16[4,5120]{1,0:T(4,128)(2,1)} %tok_ref.1, s32[4,6]{1,0:T(4,128)} %ids_ref.1, f32[4,6]{1,0:T(4,128)} %route_ref.1, s32[4]{0:T(128)} %mate_ref.1, bf16[2,96,5120]{2,1,0:T(8,128)(2,1)} %bitcast.5, bf16[8,96]{1,0:T(8,128)(2,1)} %bitcast.7, bf16[8,320]{1,0:T(8,128)(2,1)} %bitcast.6), custom_call_target="tpu_custom_call" | custom-call | tf_op jit(solution)/shard_map/lorra_step/pallas_call | solution.py:695
  112.0 1.3 %part.1 = (f32[8,96]{1,0:T(8,128)}, f32[8,320]{1,0:T(8,128)}) custom-call(f32[8,512]{1,0:T(8,128)} %lorra_step.1.both_ref), custom_call_target="tpu_custom_call" | custom-call | tf_op jit(solution)/shard_map/part/pallas_call | solution.py:743

commit v5 on v4

--- a/solution.py
+++ b/solution.py
@@ -11,7 +11,7 @@
 SCALE = 2.0
 CONTROL = 0.5
 SIDE = 4
-SHARE = 1536
+SHARE = 1024
 HIGH = lax.Precision.HIGHEST
 MESH = pl.DeviceIdType.MESH
 F32 = jnp.float32
@@ -390,45 +390,81 @@
         rows_r = slice(r * qrows, (r + 1) * qrows)
         xg[rows_r, 0:part] = xf[rows_r, 0:part].astype(BF16)
 
+    def panel(block, at):
+        return [dot_t(block, wbuf[g, :, at]) for g in range(2)]
+
+    chunk = d_half
+    rows = SIDE * tokens
+
+    def multiply(h, db):
+        by, bx = place(h, 0, db)
+
+        def step(i, carry):
+            at = pl.ds(pl.multiple_of(h * d_half + i * chunk, 128), chunk)
+            if h == 0:
+                block = xall[by, :, :, at]
+            else:
+                block = xall[:, bx, :, at]
+            for acc, value in zip((accg, accu), panel(block.reshape(rows, chunk), at)):
+                value = value.reshape(SIDE, tokens, 2 * units)
+                if h == 0:
+                    acc[by] = acc[by] + value
+                else:
+                    acc[:, bx] = acc[:, bx] + value
+            return carry
+
+        lax.fori_loop(0, d_half // chunk, step, 0)
+
+    def multiply_q():
+        at = pl.ds(part, share)
+
+        def step(i, carry):
+            block = xall[i, :, :, at].reshape(rows, share)
+            for acc, value in zip((accg, accu), panel(block, at)):
+                acc[i] = acc[i] + value.reshape(SIDE, tokens, 2 * units)
+            return carry
+
+        lax.fori_loop(0, SIDE, step, 0)
+
     a_hop(0)
-    xy_near(0)
     hop(3)
     mine_q.wait()
     lax.fori_loop(1, groups, wait_spread, 0)
     ring(0)
+    xy_near(0)
     a_hop(1)
+    hop(4)
     xy_far(0)
-    hop(4)
-    xy_pass(0, 0)
     a_hop(2)
     hop(5)
     bring(1)
     own1 = xy_own(1)
     ring(1)
-    xy_pass(0, 1)
+    xy_pass(0, 0)
     a_hop(3)
     hop(6)
+    xy_pass(0, 1)
+    ring(2)
     xy_near(1)
-    ring(2)
-    xy_pass(0, 2)
     a_hop(4)
     hop(7)
-    xy_far(1)
+    xy_pass(0, 2)
     ring(3)
-    xy_pass(0, 3)
     a_hop(5)
     hop(8)
     bring(2)
     bring(3)
     own2 = xy_own(2)
+    xy_far(1)
     for r in range(nq):
         for k in range(qz):
             at = (r * qz + k) * count
             xt[at : at + count, :] = zg[quads[r] * qz + k, :, part : part + 128].astype(F32)
     tab[...] = xt[...].astype(BF16)
+    xy_pass(0, 3)
     xy_pass(1, 0)
+    ring(4)
     a_hop(6)
-    ring(4)
     xy_near(2)
     xy_pass(1, 1)
     a_hop(7)
@@ -444,43 +480,6 @@
         copy.wait()
     xy_pass(1, 2)
     xy_pass(1, 3)
-
-    def panel(block, at):
-        return [dot_t(block, wbuf[g, :, at]) for g in range(2)]
-
-    chunk = d_half
-    rows = SIDE * tokens
-
-    def multiply(h, db):
-        by, bx = place(h, 0, db)
-
-        def step(i, carry):
-            at = pl.ds(pl.multiple_of(h * d_half + i * chunk, 128), chunk)
-            if h == 0:
-                block = xall[by, :, :, at]
-            else:
-                block = xall[:, bx, :, at]
-            for acc, value in zip((accg, accu), panel(block.reshape(rows, chunk), at)):
-                value = value.reshape(SIDE, tokens, 2 * units)
-                if h == 0:
-                    acc[by] = acc[by] + value
-                else:
-                    acc[:, bx] = acc[:, bx] + value
-            return carry
-
-        lax.fori_loop(0, d_half // chunk, step, 0)
-
-    def multiply_q():
-        at = pl.ds(part, share)
-
-        def step(i, carry):
-            block = xall[i, :, :, at].reshape(rows, share)
-            for acc, value in zip((accg, accu), panel(block, at)):
-                acc[i] = acc[i] + value.reshape(SIDE, tokens, 2 * units)
-            return carry
-
-        lax.fori_loop(0, SIDE, step, 0)
-
     xy_pass(2, 0)
     ring(6)
     gsend[...] = dot_t(apair[...], aall[...].reshape(wide, aw)).astype(BF16)
@@ -493,16 +492,17 @@
     for h in range(2):
         xy_last(1, h)
     xy_pass(2, 3)
+    multiply(0, -1)
+    multiply(0, 1)
+    multiply(1, -1)
+    multiply(1, 1)
     ring(8)
-    for h in range(2):
-        multiply(h, -1)
-        multiply(h, 1)
     multiply_q()
     gmat = lax.fori_loop(1, groups, wait_g, gsend[...].astype(F32))
-    for h in range(2):
-        xy_last(2, h)
-        multiply(h, 2)
-
+    xy_last(2, 0)
+    multiply(0, 2)
+    xy_last(2, 1)
+    multiply(1, 2)
     both = accg.shape[3]
     gate = accg[...].reshape(groups * tokens, both)
     hid[...] = (gate * (1.0 / (1.0 + jnp.exp(-gate))) * accu[...].reshape(groups * tokens, both)).astype(BF16)
@@ -551,8 +551,7 @@
         )
 
     steady = shuffle(summed[:, 0:tokens], (0, 1, 3, 2), (0, 2, 3, 1))
-    lown[:, 0:tokens] = steady[0:8]
-    lown[:, 64 : 64 + tokens] = steady[8:16]
+    lown[...] = jnp.concatenate([steady[0:8], steady[8:16]], axis=1).astype(BF16)
 
     def z_copy(k):
         return pltpu.make_async_remote_copy(
@@ -586,10 +585,10 @@
 
     for rho in range(nq):
         there = pl.ds(qz * lax.rem(a + rho, nq), qz)
-        found = lowz[there]
+        found = lowz[there].astype(F32)
         turn = qrows * rho
         for o in range(2):
-            lanes = found[:, :, 64 * o : 64 * o + tokens]
+            lanes = found[:, :, tokens * o : tokens * (o + 1)]
             if turn:
                 lanes = jnp.concatenate([lanes[:, :, tokens - turn :], lanes[:, :, : tokens - turn]], axis=2)
             val[there, 8 * o : 8 * o + 8, 0:tokens] = lanes
@@ -719,8 +718,8 @@
             pltpu.VMEM((groups * gtok, 2 * units), BF16),
             pltpu.VMEM((groups, 16, 128), F32),
             pltpu.VMEM((groups, 16, 128), F32),
-            pltpu.VMEM((8, 128), F32),
-            pltpu.VMEM((zs, 8, 128), F32),
+            pltpu.VMEM((8, 2 * gtok), BF16),
+            pltpu.VMEM((zs, 8, 2 * gtok), BF16),
             pltpu.VMEM((zs, 16, 128), F32),
             pltpu.VMEM((wide, 128), F32),
             pltpu.VMEM((16, mw), BF16),

time: 114 us -> 110 us (0.965)
  Pallas kernels: 113 us -> 109 us
    pallas_call x1, Pallas kernels: 111 us -> 108 us  [body(): pl.pallas_call(functools.partial(step_kernel, zs, total, share), out_shap...]
where the time goes in v5:
time: 110 us
  Pallas kernels  109 us (99%)
    pallas_call x1, Pallas kernels, body(): pl.pallas_call(functools.partial(step_kernel, zs, total, share), out_shap...  108 us

profile of v5, /device:TPU:1, one launch (start us, length us, event | category | flops | bytes accessed | tf_op | source)
XLA Modules:
  0.0 110.0 jit_solution(13983291451924969740)
XLA Ops:
  0.6 108.0 %lorra_step.1.both_ref = f32[8,512]{1,0:T(8,128)} custom-call(bf16[4,5120]{1,0:T(4,128)(2,1)} %tok_ref.1, s32[4,6]{1,0:T(4,128)} %ids_ref.1, f32[4,6]{1,0:T(4,128)} %route_ref.1, s32[4]{0:T(128)} %mate_ref.1, bf16[2,96,5120]{2,1,0:T(8,128)(2,1)} %bitcast.5, bf16[8,96]{1,0:T(8,128)(2,1)} %bitcast.7, bf16[8,320]{1,0:T(8,128)(2,1)} %bitcast.6), custom_call_target="tpu_custom_call" | custom-call | tf_op jit(solution)/shard_map/lorra_step/pallas_call | solution.py:694
  108.7 1.3 %part.1 = (f32[8,96]{1,0:T(8,128)}, f32[8,320]{1,0:T(8,128)}) custom-call(f32[8,512]{1,0:T(8,128)} %lorra_step.1.both_ref), custom_call_target="tpu_custom_call" | custom-call | tf_op jit(solution)/shard_map/part/pallas_call | solution.py:742

commit v6 on v5

--- a/solution.py
+++ b/solution.py
@@ -31,10 +31,10 @@
 def step_kernel(
     zs, total, share, tok_ref, ids_ref, route_ref, mate_ref, w_ref, adn_ref, aup_ref, out_ref,
     zg, zq, xf, xt, xg, tab, pk, pks, apair, apad, aall, bd, gsend, grecv,
-    xall, wbuf, accg, accu, hid, lowp, lowr, lown, lowz, val, ct, msgs, met, cot, chat, half, taken,
+    xall, wbuf, accg, accu, hid, lowp, lowr, lown, lowz, val, ct, msgs, met, cot, chat, hsend, hgot, xgot, flipped,
     ssem, rsem, lsem, wssem, wrsem, asend, arecv, rsend, rrecv, lsend, lrecv, qsend, qrecv,
     pssend, psrecv, prsend, prrecv,
-    azsend, azrecv, gssem, grsem, psend, precv, zsend, zrecv, msend, mrecv, csend, crecv,
+    azsend, azrecv, gssem, grsem, psend, precv, zsend, zrecv, msend, mrecv, csend, crecv, xsend, xrecv,
 ):
     count, d_model = tok_ref.shape
     part = d_model - share
@@ -74,7 +74,13 @@
         return carry
 
     lax.fori_loop(1, zs, greet_z, 0)
-    pl.semaphore_signal(barrier, inc=1, device_id={"expert": other}, device_id_type=MESH)
+    def greet_across(k, carry):
+        pl.semaphore_signal(
+            barrier, inc=1, device_id={"dp": lax.rem(dp + k, groups), "expert": other}, device_id_type=MESH
+        )
+        return carry
+
+    lax.fori_loop(0, groups, greet_across, 0)
     lax.fori_loop(1, groups, greet_dp, 0)
 
     weights = []
@@ -107,7 +113,7 @@
     accg[...] = jnp.zeros_like(accg)
     accu[...] = jnp.zeros_like(accu)
 
-    pl.semaphore_wait(barrier, groups + zs - 1)
+    pl.semaphore_wait(barrier, 2 * groups + zs - 2)
 
     def zdev(step):
         return {"expert": 2 * lax.rem(z + step + zs, zs) + c}
@@ -503,10 +509,15 @@
     multiply(0, 2)
     xy_last(2, 1)
     multiply(1, 2)
+    strip = pl.ds(pl.multiple_of(2 * width * (dp // 2), 128), 2 * width)
+    x_over = pltpu.make_async_remote_copy(
+        src_ref=xall.at[:, :, :, strip], dst_ref=xgot, send_sem=xsend, recv_sem=xrecv,
+        device_id={"expert": other}, device_id_type=MESH,
+    )
+    x_over.start()
     both = accg.shape[3]
     gate = accg[...].reshape(groups * tokens, both)
     hid[...] = (gate * (1.0 / (1.0 + jnp.exp(-gate))) * accu[...].reshape(groups * tokens, both)).astype(BF16)
-    strip = pl.ds(pl.multiple_of(2 * width * (dp // 2), 128), 2 * width)
     low = dot_t(bd[...], hid[...])
     tall = dot_t(apad[...], xall[:, :, :, strip].reshape(groups * tokens, 2 * width))
     for k in range(groups):
@@ -529,6 +540,14 @@
         return carry + lowr[k]
 
     lax.fori_loop(1, groups, start_low, 0)
+    hsend[:, 0:units] = hid[:, units : 2 * units]
+    h_over = pltpu.make_async_remote_copy(
+        src_ref=hsend, dst_ref=hgot, send_sem=csend, recv_sem=crecv,
+        device_id={"expert": other}, device_id_type=MESH,
+    )
+    h_over.start()
+    slabs = aall[...].astype(F32)
+    flipped[...] = jnp.concatenate([slabs[:, 8:16], slabs[:, 0:8]], axis=1).astype(BF16)
     row = lax.broadcasted_iota(jnp.int32, (wide, 128), 0)
     lane = lax.broadcasted_iota(jnp.int32, (wide, 128), 1)
     chooser = jnp.where((row // 8 == lax.rem(lane, experts)) & (lane < 3 * experts), 1.0, 0.0).astype(BF16)
@@ -601,25 +620,35 @@
     inner = jnp.dot(gmat, values, precision=HIGH, preferred_element_type=F32)
     first = weight * (factor * (SCALE * inner - CONTROL * zt))
     second = jnp.dot(mine, q, precision=HIGH, preferred_element_type=F32)
-    msgs[:, 0 : 2 * tokens] = jnp.concatenate([first, second], axis=1).astype(BF16)
-    msgs[:, 2 * tokens : 2 * tokens + wide] = dot_t(mine, values, precision=HIGH).astype(BF16)
-
-    def m_copy(k):
-        return pltpu.make_async_remote_copy(
-            src_ref=msgs, dst_ref=met.at[k], send_sem=msend.at[k], recv_sem=mrecv.at[k],
-            device_id={"dp": lax.rem(dp + k, groups)}, device_id_type=MESH,
+    third = dot_t(mine, values, precision=HIGH)
+    for o in range(2):
+        part_of = slice(8 * o, 8 * o + 8)
+        msgs[o, :, 0 : 2 * tokens] = jnp.concatenate([first[part_of], second[part_of]], axis=1).astype(BF16)
+        msgs[o, :, 2 * tokens : 2 * tokens + wide] = third[part_of].astype(BF16)
+
+    def m_copy(o, k):
+        peer = lax.rem(dp + k, groups)
+        return pltpu.make_async_remote_copy(
+            src_ref=msgs.at[o], dst_ref=met.at[o, k],
+            send_sem=msend.at[o * groups + k], recv_sem=mrecv.at[o * groups + k],
+            device_id={"dp": peer, "expert": other} if o else {"dp": peer}, device_id_type=MESH,
         )
 
     def start_m(k, carry):
-        m_copy(k).start()
+        m_copy(0, k).start()
+        m_copy(1, k).start()
         return carry
 
     def wait_m(k, carry):
-        m_copy(k).wait()
-        return carry + met[k, :, 2 * tokens : 2 * tokens + wide].astype(F32)
-
+        out = []
+        for o in range(2):
+            m_copy(o, k).wait()
+            out.append(carry[o] + met[o, k, :, 2 * tokens : 2 * tokens + wide].astype(F32))
+        return tuple(out)
+
+    m_copy(1, 0).start()
     lax.fori_loop(1, groups, start_m, 0)
-    met[0] = msgs[...]
+    met[0, 0] = msgs[0]
     lax.fori_loop(1, zs, done_z, 0)
     for step in (1, -1):
         for s in range(reach[step]):
@@ -637,33 +666,36 @@
     lax.fori_loop(1, groups, done_spread, 0)
     for copy in started:
         copy.wait_send()
-    gram = lax.fori_loop(1, groups, wait_m, msgs[:, 2 * tokens : 2 * tokens + wide].astype(F32))
-    for k in range(groups):
-        block = met[lax.rem(dp - k + groups, groups), :, 0 : 2 * tokens].astype(F32)
-        cot[:, k * tokens : (k + 1) * tokens] = block[:, 0:tokens]
-        chat[:, k * tokens : (k + 1) * tokens] = block[:, tokens : 2 * tokens]
-
-    down = SCALE * jnp.dot(cot[...].astype(BF16), hid[...], preferred_element_type=F32)
-    along = jnp.dot(
-        chat[...].astype(BF16), xall[:, :, :, strip].reshape(groups * tokens, 2 * width),
-        preferred_element_type=F32,
+    x_over.wait()
+    h_over.wait()
+    m_copy(1, 0).wait()
+    grams = lax.fori_loop(
+        1, groups, wait_m, tuple(met[o, 0, :, 2 * tokens : 2 * tokens + wide].astype(F32) for o in range(2))
     )
+    for o in range(2):
+        for k in range(groups):
+            block = met[o, lax.rem(dp - k + groups, groups), :, 0 : 2 * tokens].astype(F32)
+            cot[o, :, k * tokens : (k + 1) * tokens] = block[:, 0:tokens]
+            chat[o, :, k * tokens : (k + 1) * tokens] = block[:, tokens : 2 * tokens]
+
+    def plain(left, right):
+        return jnp.dot(left, right, preferred_element_type=F32)
+
+    down = SCALE * (
+        plain(cot[0].astype(BF16), hid[...])[:, 0:units] + plain(cot[1].astype(BF16), hgot[...])[:, 0:units]
+    )
+    along = plain(
+        chat[0].astype(BF16), xall[:, :, :, strip].reshape(groups * tokens, 2 * width)
+    ) + plain(chat[1].astype(BF16), xgot[...].reshape(groups * tokens, 2 * width))
     along = jnp.where(lax.rem(dp, 2) == 0, along[:, 0:width], along[:, width : 2 * width])
-    slices = aall[...].reshape(wide, aw)
-    hi, lo = split(gram)
-    through = jnp.dot(hi, slices, preferred_element_type=F32) + jnp.dot(lo, slices, preferred_element_type=F32)
+    through = jnp.zeros((8, aw), F32)
+    for gram, slices in zip(grams, (aall, flipped)):
+        for piece in split(gram):
+            through = through + plain(piece, slices[...].reshape(wide, aw))
     up = (SCALE * factor) * (SCALE * through[:, 0:width] - CONTROL * along)
-    half[:, 0:units] = down[8:16, units : 2 * units]
-    half[:, 128 : 128 + width] = up[8:16, :]
-    swap = pltpu.make_async_remote_copy(
-        src_ref=half, dst_ref=taken, send_sem=csend, recv_sem=crecv,
-        device_id={"expert": other}, device_id_type=MESH,
-    )
-    swap.start()
-    swap.wait()
     out_ref[...] = jnp.zeros_like(out_ref)
-    out_ref[:, 0:units] = down[0:8, 0:units] + taken[:, 0:units]
-    out_ref[:, 128 : 128 + width] = up[0:8, :] + taken[:, 128 : 128 + width]
+    out_ref[:, 0:units] = down
+    out_ref[:, 128 : 128 + width] = up
 
 
 def part_kernel(both_ref, down_ref, up_ref):
@@ -722,17 +754,19 @@
             pltpu.VMEM((zs, 8, 2 * gtok), BF16),
             pltpu.VMEM((zs, 16, 128), F32),
             pltpu.VMEM((wide, 128), F32),
-            pltpu.VMEM((16, mw), BF16),
-            pltpu.VMEM((groups, 16, mw), BF16),
-            pltpu.VMEM((16, groups * gtok), F32),
-            pltpu.VMEM((16, groups * gtok), F32),
-            pltpu.VMEM((8, 128 + aw), F32),
-            pltpu.VMEM((8, 128 + aw), F32),
+            pltpu.VMEM((2, 8, mw), BF16),
+            pltpu.VMEM((2, groups, 8, mw), BF16),
+            pltpu.VMEM((2, 8, groups * gtok), F32),
+            pltpu.VMEM((2, 8, groups * gtok), F32),
+            pltpu.VMEM((groups * gtok, 128), BF16),
+            pltpu.VMEM((groups * gtok, 128), BF16),
+            pltpu.VMEM((SIDE, SIDE, gtok, 2 * width), BF16),
+            pltpu.VMEM((zs, 16, aw), BF16),
             dma((120,)), dma((120,)), dma((6,)), dma((2,)), dma((2,)), dma, dma,
             dma((zs,)), dma((zs,)), dma((zs,)), dma((zs,)), dma((qz,)), dma((qz,)),
             dma((groups,)), dma((groups,)), dma((2 * zs,)), dma((2 * zs,)),
             dma((zs,)), dma((zs,)), dma((groups,)), dma((groups,)), dma((groups,)), dma((groups,)),
-            dma((zs,)), dma((zs,)), dma((groups,)), dma((groups,)), dma, dma,
+            dma((zs,)), dma((zs,)), dma((2 * groups,)), dma((2 * groups,)), dma, dma, dma, dma,
         ],
         compiler_params=pltpu.CompilerParams(
             collective_id=0, has_side_effects=True, vmem_limit_bytes=56 << 20

time: 110 us -> 110 us (level)
  no operation moved by 1% of the time
where the time goes in v6:
time: 110 us; the launch traced here: 109 us
  Pallas kernels  109 us (99%)
    pallas_call x1, Pallas kernels, body(): pl.pallas_call(functools.partial(step_kernel, zs, total, share), out_shap...  107 us

profile of v6, /device:TPU:1, one launch (start us, length us, event | category | flops | bytes accessed | tf_op | source)
XLA Modules:
  0.0 109.3 jit_solution(10791515759792840997)
XLA Ops:
  0.6 107.3 %lorra_step.1.both_ref = f32[8,512]{1,0:T(8,128)} custom-call(bf16[4,5120]{1,0:T(4,128)(2,1)} %tok_ref.1, s32[4,6]{1,0:T(4,128)} %ids_ref.1, f32[4,6]{1,0:T(4,128)} %route_ref.1, s32[4]{0:T(128)} %mate_ref.1, bf16[2,96,5120]{2,1,0:T(8,128)(2,1)} %bitcast.5, bf16[8,96]{1,0:T(8,128)(2,1)} %bitcast.7, bf16[8,320]{1,0:T(8,128)(2,1)} %bitcast.6), custom_call_target="tpu_custom_call" | custom-call | tf_op jit(solution)/shard_map/lorra_step/pallas_call | solution.py:726
  108.0 1.3 %part.1 = (f32[8,96]{1,0:T(8,128)}, f32[8,320]{1,0:T(8,128)}) custom-call(f32[8,512]{1,0:T(8,128)} %lorra_step.1.both_ref), custom_call_target="tpu_custom_call" | custom-call | tf_op jit(solution)/shard_map/part/pallas_call | solution.py:776

commit v7 on v6

--- a/solution.py
+++ b/solution.py
@@ -490,11 +490,11 @@
     ring(6)
     gsend[...] = dot_t(apair[...], aall[...].reshape(wide, aw)).astype(BF16)
     lax.fori_loop(1, groups, start_g, 0)
-    multiply(0, 0)
     xy_pass(2, 1)
     ring(7)
+    xy_pass(2, 2)
+    multiply(0, 0)
     multiply(1, 0)
-    xy_pass(2, 2)
     for h in range(2):
         xy_last(1, h)
     xy_pass(2, 3)

time: 110 us -> 110 us (level)
  no operation moved by 1% of the time
where the time goes in v7:
time: 110 us
  Pallas kernels  109 us (99%)
    pallas_call x1, Pallas kernels, body(): pl.pallas_call(functools.partial(step_kernel, zs, total, share), out_shap...  108 us

profile of v7, /device:TPU:1, one launch (start us, length us, event | category | flops | bytes accessed | tf_op | source)
XLA Modules:
  0.0 109.5 jit_solution(4409948179993427318)
XLA Ops:
  0.6 107.5 %lorra_step.1.both_ref = f32[8,512]{1,0:T(8,128)} custom-call(bf16[4,5120]{1,0:T(4,128)(2,1)} %tok_ref.1, s32[4,6]{1,0:T(4,128)} %ids_ref.1, f32[4,6]{1,0:T(4,128)} %route_ref.1, s32[4]{0:T(128)} %mate_ref.1, bf16[2,96,5120]{2,1,0:T(8,128)(2,1)} %bitcast.5, bf16[8,96]{1,0:T(8,128)(2,1)} %bitcast.7, bf16[8,320]{1,0:T(8,128)(2,1)} %bitcast.6), custom_call_target="tpu_custom_call" | custom-call | tf_op jit(solution)/shard_map/lorra_step/pallas_call | solution.py:726
  108.2 1.3 %part.1 = (f32[8,96]{1,0:T(8,128)}, f32[8,320]{1,0:T(8,128)}) custom-call(f32[8,512]{1,0:T(8,128)} %lorra_step.1.both_ref), custom_call_target="tpu_custom_call" | custom-call | tf_op jit(solution)/shard_map/part/pallas_call | solution.py:776
